TPU v7x, 512 devices: a whole 4x4x16 slice. The times are simulated.
512 devices in a mesh: lon: 64 (over z, x), lat: 8 (over y, core).
Axes of the slice: x: 4, y: 4, z: 16, core: 2. Of those that a mesh axis runs over, the one named last changes fastest.
Arguments:
- wet_mask: int32 [4096, 8192], P('lat', 'lon'), may hold values 0 or 1
- east_level: int32 [4096, 8192], P('lat', 'lon'), may hold values from 0 to 8
- north_level: int32 [4096, 8192], P('lat', 'lon'), may hold values from 0 to 8, as said below
- courant: float32 [4096, 8192], P('lat', 'lon'), may hold values from 0.1 to 0.45
- increment: float32 [4096, 8192], P('lat', 'lon'), may hold values from -6 to 6
- innovation: float32 [4096, 8192], P('lat', 'lon'), may hold values from -6 to 6
- obs_weight: float32 [4096, 8192], P('lat', 'lon'), may hold values from 0.2 to 2
- smooth_scale: float32 [4096], P('lat'), may hold values from 2.5 to 10
Outputs:
- final_eta: float32 [4096, 8192], P('lat', 'lon')
- precond_grad: float32 [4096, 8192], P('lat', 'lon')
Inputs may be any that keep to these rules, and one draw needn't show every extreme that they name: `north_level`: on the top row every north face is open at least half of 8 levels.
All inputs are finite; a program needn't handle non-finite values. No bound on the sum of `wet_mask` on one device may be relied on, other than what follows from the above.
Results may differ from a plain program's by a relative error of at most 0.00023.
Values sent between devices are 32-bit elements; how exact they have to be, the bound alone decides.
A program may use at most 64 MiB of HBM per device.

v0:
```python
import jax
import jax.numpy as jnp
from jax import lax
from jax.sharding import PartitionSpec as P

SUBSTEPS = 4
WLEV = 8


def with_halo(block, sides, width):
    for axis, dim in sides:
        count = lax.axis_size(axis)
        forward = [(i, i + 1) for i in range(count - 1)]
        forward.append((count - 1, 0))
        backward = [(target, source) for source, target in forward]
        low = lax.ppermute(
            lax.slice_in_dim(block, block.shape[dim] - width, None, axis=dim), axis, forward
        )
        high = lax.ppermute(lax.slice_in_dim(block, 0, width, axis=dim), axis, backward)
        block = jnp.concatenate([low, block, high], axis=dim)
    return block


def shifted(value, axis, steps):
    count = lax.axis_size(axis)
    pairs = [(source, (source + steps) % count) for source in range(count)]
    return lax.ppermute(value, axis, pairs)


def passed_along(value, axis, steps):
    count = lax.axis_size(axis)
    leading, last = (max(0, -steps), min(count, count - steps))
    return lax.ppermute(value, axis, [(source, source + steps) for source in range(leading, last)])


def shift_cols(values, stride, eastward):
    if eastward:
        return jnp.pad(values[..., :-stride], ((0, 0), (0, 0), (stride, 0)))
    return jnp.pad(values[..., stride:], ((0, 0), (0, 0), (0, stride)))


def block_cycle(east_end, west_end, block_decay):
    east_sum = east_end
    west_sum = west_end
    weight = block_decay
    blocks_all = east_end.shape[1]
    for bit_index in range(blocks_all.bit_length() - 1):
        stride = 2**bit_index
        east_sum = east_sum + weight * jnp.roll(east_sum, stride, axis=1)
        west_sum = west_sum + weight * jnp.roll(west_sum, -stride, axis=1)
        weight = weight * weight
    return (east_sum, west_sum, blocks_all)


def zonal_solve(source, stiffness, cycle):
    width = source.shape[-1]
    stiff_rows = stiffness[:, None, None]
    root_term = jnp.sqrt(1.0 + 4.0 * stiff_rows)
    log_root = jnp.log1p(-(root_term - 1.0) / (2.0 * stiff_rows))
    green_scale = 1.0 / root_term
    forward_sum = source
    backward_sum = source
    stride = 1
    while stride < width:
        factor = jnp.exp(float(stride) * log_root)
        forward_sum = forward_sum + factor * shift_cols(forward_sum, stride, True)
        backward_sum = backward_sum + factor * shift_cols(backward_sum, stride, False)
        stride = stride * 2
    row_log = log_root[..., 0]
    block_decay = jnp.exp(float(width) * row_log)
    east_end = forward_sum[..., -1]
    west_end = backward_sum[..., 0]
    east_sum, west_sum, blocks_all = cycle(east_end, west_end, block_decay)
    wrap_weight = jnp.exp(float((blocks_all - 1) * width) * row_log)
    image_sum = 1.0 - jnp.exp(float(blocks_all * width) * row_log)
    east_in = ((east_sum - east_end) / block_decay + wrap_weight * east_end) / image_sum
    west_in = ((west_sum - west_end) / block_decay + wrap_weight * west_end) / image_sum
    column = jnp.arange(width, dtype=jnp.float32)
    forward_all = forward_sum + jnp.exp((column + 1.0) * log_root) * east_in[..., None]
    backward_all = backward_sum + jnp.exp((float(width) - column) * log_root) * west_in[..., None]
    return green_scale * (forward_all + backward_all - source)


def mirror_row(values, col_count):
    gathered = lax.all_gather(values, "lon", axis=0, tiled=True)
    return lax.dynamic_slice_in_dim(gathered[::-1], lax.axis_index("lon") * col_count, col_count)


def laplace(state_now, face_set, at_top):
    east_face, west_face, north_face, south_face = face_set
    padded = with_halo(state_now, (("lat", 0), ("lon", 1)), 1)
    folded = mirror_row(state_now[-1], state_now.shape[1])
    north_vals = padded[2:, 1:-1]
    north_vals = north_vals.at[-1].set(jnp.where(at_top, folded, north_vals[-1]))
    return (
        east_face * (padded[1:-1, 2:] - state_now)
        + west_face * (padded[1:-1, :-2] - state_now)
        + north_face * (north_vals - state_now)
        + south_face * (padded[:-2, 1:-1] - state_now)
    )


def local(
    wet_mask, east_level, north_level, courant, increment, innovation, obs_weight, smooth_scale
):
    row_count, col_count = increment.shape
    lon_count = lax.axis_size("lon")
    at_top = lax.axis_index("lat") == lax.axis_size("lat") - 1
    wet_frac = wet_mask.astype(jnp.float32)
    east_face = east_level.astype(jnp.float32) / WLEV
    raw_north = north_level.astype(jnp.float32) / WLEV
    west_edge = shifted(east_face[:, -1], "lon", 1)
    west_face = jnp.concatenate([west_edge[:, None], east_face[:, :-1]], axis=1)
    south_edge = passed_along(raw_north[-1], "lat", 1)
    south_face = jnp.concatenate([south_edge[None], raw_north[:-1]], axis=0)
    top_faces = raw_north[-1]
    fold_face = top_faces * mirror_row(top_faces, col_count)
    north_face = raw_north.at[-1].set(jnp.where(at_top, fold_face, top_faces))
    face_set = (east_face, west_face, north_face, south_face)
    state_now = wet_frac * increment
    before = state_now
    for substep in range(SUBSTEPS):
        after = 2.0 * state_now - before + wet_frac * courant * laplace(state_now, face_set, at_top)
        before = state_now
        state_now = after
    adjoint = wet_frac * obs_weight * (state_now - innovation)
    carried = jnp.zeros_like(adjoint)
    for substep in range(SUBSTEPS):
        updated = (
            2.0 * adjoint
            + wet_frac * laplace(courant * wet_frac * adjoint, face_set, at_top)
            + carried
        )
        carried = -adjoint
        adjoint = updated
    gradient = wet_frac * (adjoint + carried)
    lines = lax.all_to_all(gradient, "lon", split_axis=0, concat_axis=1, tiled=True)
    line_rows = row_count // lon_count
    row_scales = lax.dynamic_slice_in_dim(
        smooth_scale, lax.axis_index("lon") * line_rows, line_rows
    )
    stiffness = row_scales * float(col_count * col_count)
    blocked = lines.reshape(line_rows, lon_count, col_count)
    smoothed = zonal_solve(blocked, stiffness, block_cycle).reshape(
        line_rows, lon_count * col_count
    )
    smoothed = smoothed * (2.0 * stiffness**0.25)[:, None]
    precond_grad = lax.all_to_all(smoothed, "lon", split_axis=1, concat_axis=0, tiled=True)
    return (state_now, precond_grad)


def solution(mesh):
    return jax.shard_map(
        local,
        mesh=mesh,
        in_specs=(
            P("lat", "lon"),
            P("lat", "lon"),
            P("lat", "lon"),
            P("lat", "lon"),
            P("lat", "lon"),
            P("lat", "lon"),
            P("lat", "lon"),
            P("lat"),
        ),
        out_specs=(P("lat", "lon"), P("lat", "lon")),
        check_vma=False,
    )
```

profile of v0, /device:TPU:2, one launch (start us, length us, event | category | flops | bytes accessed | tf_op | source)
XLA Modules:
  0.0 885.1 jit_solution(8038742436026527924)
XLA Ops:
  0.6 1.1 convert_multiply_fusion.3
  1.8 2.9 collective-permute-start.1
  4.8 1.3 collective-permute-start.5
  6.3 3.4 collective-permute-start.3
  9.7 79.2 %all-gather = f32[1,8192]{1,0:T(1,128)S(1)} all-gather(f32[1,128]{1,0:T(1,128)S(1)} %get-tuple-element.160), channel_id=2, replica_groups=mesh['lon'=64,'lat'=8] {'lon'}, dimensions={1}, use_global_device_ids=true | all-gather | bytes 33280 | tf_op jit(solution)/shard_map/all_gather | solution.py:85
  89.1 72.9 %all-gather.1 = f32[1,8192]{1,0:T(1,128)S(1)} all-gather(f32[1,128]{1,0:T(1,128)S(1)} %get-tuple-element.162), channel_id=3, replica_groups=mesh['lon'=64,'lat'=8] {'lon'}, dimensions={1}, use_global_device_ids=true | all-gather | bytes 33280 | tf_op jit(solution)/shard_map/all_gather | solution.py:85
  163.0 2.9 collective-permute-start.4
  165.9 2.9 collective-permute-start.2
  169.2 2.3 collective-permute-done.4
  171.5 2.7 collective-permute-done.2
  174.2 1.4 fusion
  175.6 2.9 collective-permute-start.7
  178.5 75.9 %all-gather.2 = f32[1,8192]{1,0:T(1,128)S(1)} all-gather(f32[1,128]{1,0:T(1,128)S(1)} %get-tuple-element.158), channel_id=4, replica_groups=mesh['lon'=64,'lat'=8] {'lon'}, dimensions={1}, use_global_device_ids=true | all-gather | bytes 33280 | tf_op jit(solution)/shard_map/all_gather | solution.py:85
  255.4 2.0 collective-permute-start.9
  257.4 3.9 collective-permute-start.8
  261.4 2.5 collective-permute-done.9
  263.9 1.8 collective-permute-done.8
  266.1 2.9 collective-permute-start.11
  269.0 75.5 %all-gather.3 = f32[1,8192]{1,0:T(1,128)S(1)} all-gather(f32[1,128]{1,0:T(1,128)S(1)} %get-tuple-element.156), channel_id=5, replica_groups=mesh['lon'=64,'lat'=8] {'lon'}, dimensions={1}, use_global_device_ids=true | all-gather | bytes 33280 | tf_op jit(solution)/shard_map/all_gather | solution.py:85
  345.5 3.0 collective-permute-start.13
  348.5 2.9 collective-permute-start.12
  351.5 2.5 collective-permute-done.13
  354.1 2.8 collective-permute-done.12
  357.2 2.9 collective-permute-start.15
  360.2 75.6 %all-gather.4 = f32[1,8192]{1,0:T(1,128)S(1)} all-gather(f32[1,128]{1,0:T(1,128)S(1)} %get-tuple-element.154), channel_id=6, replica_groups=mesh['lon'=64,'lat'=8] {'lon'}, dimensions={1}, use_global_device_ids=true | all-gather | bytes 33280 | tf_op jit(solution)/shard_map/all_gather | solution.py:85
  435.8 0.9 fusion.149
  436.7 2.0 collective-permute-start.17
  438.7 3.9 collective-permute-start.16
  442.7 2.5 collective-permute-done.17
  445.2 2.0 collective-permute-done.16
  447.2 2.1 fusion.142
  449.3 3.0 collective-permute-start.19
  452.3 76.7 %all-gather.5 = f32[1,8192]{1,0:T(1,128)S(1)} all-gather(f32[1,128]{1,0:T(1,128)S(1)} %get-tuple-element.152), channel_id=7, replica_groups=mesh['lon'=64,'lat'=8] {'lon'}, dimensions={1}, use_global_device_ids=true | all-gather | bytes 33280 | tf_op jit(solution)/shard_map/all_gather | solution.py:85
  529.2 3.0 collective-permute-start.21
  532.2 2.9 collective-permute-start.20
  535.2 2.3 collective-permute-done.21
  537.5 3.1 collective-permute-done.20
  540.6 1.3 fusion.140
  542.0 2.9 collective-permute-start.23
  544.9 75.6 %all-gather.6 = f32[1,8192]{1,0:T(1,128)S(1)} all-gather(f32[1,128]{1,0:T(1,128)S(1)} %get-tuple-element.150), channel_id=8, replica_groups=mesh['lon'=64,'lat'=8] {'lon'}, dimensions={1}, use_global_device_ids=true | all-gather | bytes 33280 | tf_op jit(solution)/shard_map/all_gather | solution.py:85
  620.6 0.9 fusion.147
  621.5 2.0 collective-permute-start.25
  623.4 3.9 collective-permute-start.24
  627.5 2.5 collective-permute-done.25
  630.0 2.1 collective-permute-done.24
  632.1 1.3 fusion.138
  633.5 2.9 collective-permute-start.27
  636.4 75.5 %all-gather.7 = f32[1,8192]{1,0:T(1,128)S(1)} all-gather(f32[1,128]{1,0:T(1,128)S(1)} %get-tuple-element.148), channel_id=9, replica_groups=mesh['lon'=64,'lat'=8] {'lon'}, dimensions={1}, use_global_device_ids=true | all-gather | bytes 33280 | tf_op jit(solution)/shard_map/all_gather | solution.py:85
  712.1 0.9 fusion.146
  712.9 3.0 collective-permute-start.29
  715.9 2.9 collective-permute-start.28
  718.9 2.5 collective-permute-done.29
  721.4 3.1 collective-permute-done.28
  724.5 1.3 fusion.136
  725.9 2.9 collective-permute-start.31
  728.8 75.6 %all-gather.8 = f32[1,8192]{1,0:T(1,128)S(1)} all-gather(f32[1,128]{1,0:T(1,128)S(1)} %get-tuple-element.146), channel_id=10, replica_groups=mesh['lon'=64,'lat'=8] {'lon'}, dimensions={1}, use_global_device_ids=true | all-gather | bytes 33280 | tf_op jit(solution)/shard_map/all_gather | solution.py:85
  805.4 2.0 collective-permute-start.33
  807.3 3.9 collective-permute-start.32
  811.4 2.8 collective-permute-done.33
  814.2 1.8 collective-permute-done.32
  816.0 1.1 fusion.9
  817.0 17.4 %all-to-all-start = ((f32[64,8,128]{2,1,0:T(8,128)}), f32[64,8,128]{2,1,0:T(8,128)S(1)}, u32[]{:S(2)}, u32[]{:S(2)}) async-start(f32[64,8,128]{2,1,0:T(8,128)} %fusion.9), calls=%async_computation | async-start | bytes 524288 | tf_op jit(solution)/shard_map/all_to_all | solution.py:137
  835.4 21.2 %all-to-all-done = f32[64,8,128]{2,1,0:T(8,128)S(1)} async-done(((f32[64,8,128]{2,1,0:T(8,128)}), f32[64,8,128]{2,1,0:T(8,128)S(1)}, u32[]{:S(2)}, u32[]{:S(2)}) %all-to-all-start) | async-done | bytes 262176 | tf_op jit(solution)/shard_map/all_to_all | solution.py:137
  860.6 23.8 %all_to_all.32 = f32[8,64,128]{2,0,1:T(8,128)S(1)} all-to-all(f32[8,64,128]{2,0,1:T(8,128)S(1)} %copy.746), channel_id=1, replica_groups=mesh['lon'=64,'lat'=8] {'lon'}, dimensions={1} | all-to-all | bytes 524288 | tf_op jit(solution)/shard_map/all_to_all | solution.py:148
  (155 shorter events, 12.6 us)
Async XLA Ops:
  0.6 4.1 copy-start.2
  1.8 160.3 %collective-permute-start = (f32[1,128]{1,0:T(1,128)S(1)}, f32[1,128]{1,0:T(1,128)S(1)}, u32[]{:S(2)}, u32[]{:S(2)}) collective-permute-start(f32[1,128]{1,0:T(1,128)S(1)} %get-tuple-element.162), channel_id=1, source_target_pairs={{0,1},{1,2},{2,3},{3,4},{4,5},{5,6},{6,7},{7,0},{8,9},{9,10},{10,1... | collective-permute-start | bytes 1544 | tf_op jit(solution)/shard_map/ppermute | solution.py:16
  1.8 4.3 copy-start
  1.8 160.3 %collective-permute-start.1 = (f32[1,128]{1,0:T(1,128)S(1)}, f32[1,128]{1,0:T(1,128)S(1)}, u32[]{:S(2)}, u32[]{:S(2)}) collective-permute-start(f32[1,128]{1,0:T(1,128)S(1)} %get-tuple-element.161), channel_id=1, source_target_pairs={{1,0},{2,1},{3,2},{4,3},{5,4},{6,5},{7,6},{0,7},{9,8},{10,9},{11,1... | collective-permute-start | bytes 1544 | tf_op jit(solution)/shard_map/ppermute | solution.py:19
  4.8 164.4 %collective-permute-start.5 = (f32[128]{0:T(128)S(1)}, f32[128]{0:T(128)S(1)}, u32[]{:S(2)}, u32[]{:S(2)}) collective-permute-start(f32[128]{0:T(128)S(1)} %get-tuple-element.159), channel_id=1, source_target_pairs={{0,1},{1,2},{2,3},{3,4},{4,5},{5,6},{6,7},{8,9},{9,10},{10,11},{11... | collective-permute-start | bytes 1544 | tf_op jit(solution)/shard_map/ppermute | solution.py:33
  6.3 162.6 %collective-permute-start.3 = (f32[512]{0:T(512)S(1)}, f32[512]{0:T(512)S(1)}, u32[]{:S(2)}, u32[]{:S(2)}) collective-permute-start(f32[512]{0:T(512)S(1)} %slice_reduce_fusion), channel_id=1, source_target_pairs={{0,8},{8,16},{16,24},{24,32},{32,40},{40,48},{48,56},{56,64},{64,7... | collective-permute-start | bytes 6152 | tf_op jit(solution)/shard_map/ppermute | solution.py:27
  163.0 8.5 collective-permute-start.4
  165.9 8.3 collective-permute-start.2
  168.9 5.3 copy-start.1
  175.6 79.0 %collective-permute-start.6 = (f32[1,128]{1,0:T(1,128)S(1)}, f32[1,128]{1,0:T(1,128)S(1)}, u32[]{:S(2)}, u32[]{:S(2)}) collective-permute-start(f32[1,128]{1,0:T(1,128)S(1)} %get-tuple-element.158), channel_id=1, source_target_pairs={{0,1},{1,2},{2,3},{3,4},{4,5},{5,6},{6,7},{7,0},{8,9},{9,10},{10,1... | collective-permute-start | bytes 1544 | tf_op jit(solution)/shard_map/ppermute | solution.py:16
  175.6 78.9 %collective-permute-start.7 = (f32[1,128]{1,0:T(1,128)S(1)}, f32[1,128]{1,0:T(1,128)S(1)}, u32[]{:S(2)}, u32[]{:S(2)}) collective-permute-start(f32[1,128]{1,0:T(1,128)S(1)} %get-tuple-element.157), channel_id=1, source_target_pairs={{1,0},{2,1},{3,2},{4,3},{5,4},{6,5},{7,6},{0,7},{9,8},{10,9},{11,1... | collective-permute-start | bytes 1544 | tf_op jit(solution)/shard_map/ppermute | solution.py:19
  255.4 8.5 collective-permute-start.9
  257.4 8.3 collective-permute-start.8
  266.1 78.6 %collective-permute-start.10 = (f32[1,128]{1,0:T(1,128)S(1)}, f32[1,128]{1,0:T(1,128)S(1)}, u32[]{:S(2)}, u32[]{:S(2)}) collective-permute-start(f32[1,128]{1,0:T(1,128)S(1)} %get-tuple-element.156), channel_id=1, source_target_pairs={{0,1},{1,2},{2,3},{3,4},{4,5},{5,6},{6,7},{7,0},{8,9},{9,10},{10,1... | collective-permute-start | bytes 1544 | tf_op jit(solution)/shard_map/ppermute | solution.py:16
  266.1 78.6 %collective-permute-start.11 = (f32[1,128]{1,0:T(1,128)S(1)}, f32[1,128]{1,0:T(1,128)S(1)}, u32[]{:S(2)}, u32[]{:S(2)}) collective-permute-start(f32[1,128]{1,0:T(1,128)S(1)} %get-tuple-element.155), channel_id=1, source_target_pairs={{1,0},{2,1},{3,2},{4,3},{5,4},{6,5},{7,6},{0,7},{9,8},{10,9},{11,1... | collective-permute-start | bytes 1544 | tf_op jit(solution)/shard_map/ppermute | solution.py:19
  345.5 8.5 collective-permute-start.13
  348.5 8.3 collective-permute-start.12
  357.2 78.6 %collective-permute-start.14 = (f32[1,128]{1,0:T(1,128)S(1)}, f32[1,128]{1,0:T(1,128)S(1)}, u32[]{:S(2)}, u32[]{:S(2)}) collective-permute-start(f32[1,128]{1,0:T(1,128)S(1)} %get-tuple-element.154), channel_id=1, source_target_pairs={{0,1},{1,2},{2,3},{3,4},{4,5},{5,6},{6,7},{7,0},{8,9},{9,10},{10,1... | collective-permute-start | bytes 1544 | tf_op jit(solution)/shard_map/ppermute | solution.py:16
  357.2 78.6 %collective-permute-start.15 = (f32[1,128]{1,0:T(1,128)S(1)}, f32[1,128]{1,0:T(1,128)S(1)}, u32[]{:S(2)}, u32[]{:S(2)}) collective-permute-start(f32[1,128]{1,0:T(1,128)S(1)} %get-tuple-element.153), channel_id=1, source_target_pairs={{1,0},{2,1},{3,2},{4,3},{5,4},{6,5},{7,6},{0,7},{9,8},{10,9},{11,1... | collective-permute-start | bytes 1544 | tf_op jit(solution)/shard_map/ppermute | solution.py:19
  436.7 8.5 collective-permute-start.17
  438.7 8.5 collective-permute-start.16
  449.3 79.8 %collective-permute-start.18 = (f32[1,128]{1,0:T(1,128)S(1)}, f32[1,128]{1,0:T(1,128)S(1)}, u32[]{:S(2)}, u32[]{:S(2)}) collective-permute-start(f32[1,128]{1,0:T(1,128)S(1)} %get-tuple-element.152), channel_id=1, source_target_pairs={{0,1},{1,2},{2,3},{3,4},{4,5},{5,6},{6,7},{7,0},{8,9},{9,10},{10,1... | collective-permute-start | bytes 1544 | tf_op jit(solution)/shard_map/ppermute | solution.py:16
  449.3 79.8 %collective-permute-start.19 = (f32[1,128]{1,0:T(1,128)S(1)}, f32[1,128]{1,0:T(1,128)S(1)}, u32[]{:S(2)}, u32[]{:S(2)}) collective-permute-start(f32[1,128]{1,0:T(1,128)S(1)} %get-tuple-element.151), channel_id=1, source_target_pairs={{1,0},{2,1},{3,2},{4,3},{5,4},{6,5},{7,6},{0,7},{9,8},{10,9},{11,1... | collective-permute-start | bytes 1544 | tf_op jit(solution)/shard_map/ppermute | solution.py:19
  529.2 8.3 collective-permute-start.21
  532.2 8.4 collective-permute-start.20
  541.9 78.6 %collective-permute-start.22 = (f32[1,128]{1,0:T(1,128)S(1)}, f32[1,128]{1,0:T(1,128)S(1)}, u32[]{:S(2)}, u32[]{:S(2)}) collective-permute-start(f32[1,128]{1,0:T(1,128)S(1)} %get-tuple-element.150), channel_id=1, source_target_pairs={{0,1},{1,2},{2,3},{3,4},{4,5},{5,6},{6,7},{7,0},{8,9},{9,10},{10,1... | collective-permute-start | bytes 1544 | tf_op jit(solution)/shard_map/ppermute | solution.py:16
  542.0 78.6 %collective-permute-start.23 = (f32[1,128]{1,0:T(1,128)S(1)}, f32[1,128]{1,0:T(1,128)S(1)}, u32[]{:S(2)}, u32[]{:S(2)}) collective-permute-start(f32[1,128]{1,0:T(1,128)S(1)} %get-tuple-element.149), channel_id=1, source_target_pairs={{1,0},{2,1},{3,2},{4,3},{5,4},{6,5},{7,6},{0,7},{9,8},{10,9},{11,1... | collective-permute-start | bytes 1544 | tf_op jit(solution)/shard_map/ppermute | solution.py:19
  621.5 8.5 collective-permute-start.25
  623.4 8.7 collective-permute-start.24
  633.4 78.6 %collective-permute-start.26 = (f32[1,128]{1,0:T(1,128)S(1)}, f32[1,128]{1,0:T(1,128)S(1)}, u32[]{:S(2)}, u32[]{:S(2)}) collective-permute-start(f32[1,128]{1,0:T(1,128)S(1)} %get-tuple-element.148), channel_id=1, source_target_pairs={{0,1},{1,2},{2,3},{3,4},{4,5},{5,6},{6,7},{7,0},{8,9},{9,10},{10,1... | collective-permute-start | bytes 1544 | tf_op jit(solution)/shard_map/ppermute | solution.py:16
  633.5 78.6 %collective-permute-start.27 = (f32[1,128]{1,0:T(1,128)S(1)}, f32[1,128]{1,0:T(1,128)S(1)}, u32[]{:S(2)}, u32[]{:S(2)}) collective-permute-start(f32[1,128]{1,0:T(1,128)S(1)} %get-tuple-element.147), channel_id=1, source_target_pairs={{1,0},{2,1},{3,2},{4,3},{5,4},{6,5},{7,6},{0,7},{9,8},{10,9},{11,1... | collective-permute-start | bytes 1544 | tf_op jit(solution)/shard_map/ppermute | solution.py:19
  712.9 8.5 collective-permute-start.29
  715.9 8.6 collective-permute-start.28
  725.9 78.6 %collective-permute-start.30 = (f32[1,128]{1,0:T(1,128)S(1)}, f32[1,128]{1,0:T(1,128)S(1)}, u32[]{:S(2)}, u32[]{:S(2)}) collective-permute-start(f32[1,128]{1,0:T(1,128)S(1)} %get-tuple-element.146), channel_id=1, source_target_pairs={{0,1},{1,2},{2,3},{3,4},{4,5},{5,6},{6,7},{7,0},{8,9},{9,10},{10,1... | collective-permute-start | bytes 1544 | tf_op jit(solution)/shard_map/ppermute | solution.py:16
  725.9 78.6 %collective-permute-start.31 = (f32[1,128]{1,0:T(1,128)S(1)}, f32[1,128]{1,0:T(1,128)S(1)}, u32[]{:S(2)}, u32[]{:S(2)}) collective-permute-start(f32[1,128]{1,0:T(1,128)S(1)} %get-tuple-element.145), channel_id=1, source_target_pairs={{1,0},{2,1},{3,2},{4,3},{5,4},{6,5},{7,6},{0,7},{9,8},{10,9},{11,1... | collective-permute-start | bytes 1544 | tf_op jit(solution)/shard_map/ppermute | solution.py:19
  805.4 8.8 collective-permute-start.33
  807.3 8.6 collective-permute-start.32
  817.0 39.5 %all-to-all-start = ((f32[64,8,128]{2,1,0:T(8,128)}), f32[64,8,128]{2,1,0:T(8,128)S(1)}, u32[]{:S(2)}, u32[]{:S(2)}) async-start(f32[64,8,128]{2,1,0:T(8,128)} %fusion.9), calls=%async_computation | async-start | bytes 524288 | tf_op jit(solution)/shard_map/all_to_all | solution.py:137
where the time goes:
time: 886 us; the launch traced here: 885 us
  blocking collectives  706 us (80%)
  starting transfers between devices  92.4 us (10%)
  waiting for transfers between devices  60.6 us (7%)
  other arithmetic  14.4 us (2%)
  local copies, waits for them, and re-layouts  10.2 us (1%)
    all_gather x9, blocking collectives, mirror_row(): gathered = lax.all_gather(values, 'lon', axis=0, tiled=True)  682 us
    ppermute x16, starting transfers between devices, with_halo(): lax.ppermute(lax.slice_in_dim(block, 0, width, axis=dim), axis, backward)  50.6 us
    all_to_all x1, blocking collectives, local(): lax.all_to_all(smoothed, 'lon', split_axis=1, concat_axis=0, tiled=True)  23.8 us
    all_to_all x1, waiting for transfers between devices, local(): lax.all_to_all(gradient, 'lon', split_axis=0, concat_axis=1, tiled=True)  21.2 us
    ppermute x16, waiting for transfers between devices, with_halo(): lax.ppermute(lax.slice_in_dim(block, block.shape[dim] - width, None, axis...  20.1 us
    ppermute x16, starting transfers between devices, with_halo(): lax.ppermute(lax.slice_in_dim(block, block.shape[dim] - width, None, axis...  19.8 us
    ppermute x16, waiting for transfers between devices, with_halo(): lax.ppermute(lax.slice_in_dim(block, 0, width, axis=dim), axis, backward)  19.4 us
  transfers between devices with their start and end apart: 35, of which 17 were waited for; matrix products, arithmetic and copies ran while one was open for 0% of the time, Pallas kernels for 0%

commit v1 on v0

v1 whole, which is shorter than its diff:
```python
import functools
import jax
import jax.numpy as jnp
from jax import lax
from jax.experimental import pallas as pl
from jax.experimental.pallas import tpu as pltpu
from jax.sharding import PartitionSpec as P

SUBSTEPS = 4
WLEV = 8
F32 = jnp.float32
BF16 = jnp.bfloat16
XG = 4
FIELDS = 6
PAD = 16
RH = 48
HIGH = lax.Precision.HIGHEST


def roll(value, shift, axis):
    return pltpu.roll(value, shift % value.shape[axis], axis)


def iota(shape, dim):
    return lax.broadcasted_iota(jnp.int32, shape, dim)


def split3(value):
    high = value.astype(BF16)
    rest = value - high.astype(F32)
    mid = rest.astype(BF16)
    low = (rest - mid.astype(F32)).astype(BF16)
    return high, mid, low


def remote(src, dst, send_sem, recv_sem, lon, lat):
    return pltpu.make_async_remote_copy(
        src_ref=src,
        dst_ref=dst,
        send_sem=send_sem,
        recv_sem=recv_sem,
        device_id={"lon": lon, "lat": lat},
        device_id_type=pl.DeviceIdType.MESH,
    )


def kernel(
    nlon,
    nlat,
    wet_hbm,
    east_hbm,
    north_hbm,
    cour_hbm,
    incr_hbm,
    innov_hbm,
    ow_hbm,
    scale_ref,
    eta_hbm,
    grad_hbm,
    raw_i,
    raw_f,
    main,
    halo,
    work,
    delta,
    packed,
    strip_out,
    strip_in,
    corner,
    eta_buf,
    grad_buf,
    powers,
    gains,
    parts,
    sums,
    xbuf,
    zbuf,
    in_sem,
    out_sem,
    hs,
    hr,
    xs,
    xr,
    zs,
    zr,
):
    lon = lax.axis_index("lon")
    lat = lax.axis_index("lat")
    nz = nlon // XG
    x_pos = lax.rem(lon, XG)
    z_pos = lon // XG
    top = lat == nlat - 1
    low = lat == 0
    east_lon = lax.rem(lon + 1, nlon)
    west_lon = lax.rem(lon + nlon - 1, nlon)
    fold_lon = nlon - 1 - lon
    fold_ne = lax.rem(2 * nlon - 2 - lon, nlon)
    fold_nw = lax.rem(nlon - lon, nlon)
    ne_self = fold_ne == lon
    nw_self = fold_nw == lon

    loads = [
        pltpu.make_async_copy(wet_hbm, raw_i.at[0], in_sem.at[0]),
        pltpu.make_async_copy(cour_hbm, raw_f.at[0], in_sem.at[1]),
        pltpu.make_async_copy(incr_hbm, raw_f.at[1], in_sem.at[2]),
        pltpu.make_async_copy(east_hbm, raw_i.at[1], in_sem.at[3]),
        pltpu.make_async_copy(north_hbm, raw_i.at[2], in_sem.at[4]),
        pltpu.make_async_copy(ow_hbm, main.at[4, pl.ds(PAD, 512)], in_sem.at[5]),
        pltpu.make_async_copy(innov_hbm, main.at[5, pl.ds(PAD, 512)], in_sem.at[6]),
    ]
    for load in loads:
        load.start()

    barrier = pltpu.get_barrier_semaphore()

    def greet(to_lon, to_lat):
        pl.semaphore_signal(
            barrier,
            inc=1,
            device_id={"lon": to_lon, "lat": to_lat},
            device_id_type=pl.DeviceIdType.MESH,
        )

    def x_peer(step):
        return z_pos * XG + lax.rem(x_pos + step, XG)

    def z_peer(step):
        return lax.rem(z_pos + step, nz) * XG + x_pos

    greet(east_lon, lat)
    greet(west_lon, lat)

    @pl.when(jnp.logical_not(low))
    def _():
        greet(lon, lat - 1)
        greet(east_lon, lat - 1)
        greet(west_lon, lat - 1)

    @pl.when(jnp.logical_not(top))
    def _():
        greet(lon, lat + 1)
        greet(east_lon, lat + 1)
        greet(west_lon, lat + 1)

    @pl.when(top)
    def _():
        greet(fold_lon, lat)

        @pl.when(jnp.logical_not(ne_self))
        def _():
            greet(fold_ne, lat)

        @pl.when(jnp.logical_not(nw_self))
        def _():
            greet(fold_nw, lat)

    for step in range(1, XG):
        greet(x_peer(step), lat)
    for step in range(1, nz):
        greet(z_peer(step), lat)

    lane8 = iota((8, 128), 1)
    sub8 = iota((8, 128), 0)

    zero8 = jnp.zeros((8, 128), F32)
    zstrip = jnp.zeros((8, 512), F32)
    strip_in[0, 0] = zstrip
    strip_in[6, 1] = zstrip
    strip_in[7, 0] = zstrip
    strip_in[7, 1] = zstrip
    for edge in (0, 536):
        for field in (0, 3):
            main[field, pl.ds(edge, 8)] = zero8
            halo[field, pl.ds(edge, 8)] = zero8
        work[0, pl.ds(edge, 8)] = zero8
        work[1, pl.ds(edge, 8)] = zero8

    @pl.when(low)
    def _():
        for field in range(FIELDS):
            main[field, pl.ds(8, 8)] = zero8
        corner[0] = zero8
        corner[1] = zero8

    for load in loads:
        load.wait()
    slot = (iota((64, 128), 1) + 8) // 16

    def build(step, carry):
        row = pl.multiple_of(step * 64, 64)
        own = pl.ds(pl.multiple_of(step * 64 + PAD, 16), 64)
        rows = pl.ds(row, 64)
        wet = raw_i[0, rows].astype(F32)
        fields = [
            wet * raw_f[1, rows],
            wet * raw_f[0, rows],
            raw_i[1, rows].astype(F32) * (1.0 / WLEV),
            raw_i[2, rows].astype(F32) * (1.0 / WLEV),
        ]
        for index, value in enumerate(fields):
            main[index, own] = value
        fields.append(main[4, own])
        fields.append(main[5, own])
        joined = roll(fields[0], 16, 1)
        for index in range(1, FIELDS):
            joined = jnp.where(slot == index + 1, roll(fields[index], 16 * (index + 1), 1), joined)
        packed[rows] = joined
        return carry

    lax.fori_loop(0, 8, build, 0)

    def turn(step, carry):
        rows = pl.ds(pl.multiple_of(step * 128, 128), 128)
        strip_out[:, :, :, rows] = packed[rows].T.reshape(8, 2, 8, 128)
        return carry

    lax.fori_loop(0, 4, turn, 0)

    links = 2 + (XG - 1) + (nz - 1)
    north_links = jnp.where(
        top, 3 - ne_self.astype(jnp.int32) - nw_self.astype(jnp.int32), 3
    )
    south_links = jnp.where(low, 0, 3)
    pl.semaphore_wait(barrier, links + north_links + south_links)

    top_rows = main.at[:, pl.ds(PAD + 504, 8)]
    low_rows = main.at[:, pl.ds(PAD, 8)]
    south_halo = main.at[:, pl.ds(8, 8)]
    north_halo = main.at[:, pl.ds(PAD + 512, 8)]
    top_tile = packed.at[pl.ds(504, 8)]
    low_tile = packed.at[pl.ds(0, 8)]
    to_west = remote(
        strip_out.at[pl.ds(1, 6), 0], strip_in.at[pl.ds(1, 6), 0], hs.at[2], hr.at[3], west_lon, lat
    )
    to_east = remote(
        strip_out.at[pl.ds(0, 6), 1], strip_in.at[pl.ds(0, 6), 1], hs.at[3], hr.at[2], east_lon, lat
    )
    to_south = remote(low_rows, north_halo, hs.at[0], hr.at[1], lon, lat - 1)
    to_sw = remote(low_tile, corner.at[3], hs.at[4], hr.at[7], west_lon, lat - 1)
    to_se = remote(low_tile, corner.at[2], hs.at[5], hr.at[6], east_lon, lat - 1)
    to_north = remote(top_rows, south_halo, hs.at[1], hr.at[0], lon, lat + 1)
    to_nw = remote(top_tile, corner.at[1], hs.at[6], hr.at[5], west_lon, lat + 1)
    to_ne = remote(top_tile, corner.at[0], hs.at[7], hr.at[4], east_lon, lat + 1)
    over_fold = remote(top_rows, north_halo, hs.at[1], hr.at[1], fold_lon, lat)
    fold_to_nw = remote(top_tile, corner.at[2], hs.at[6], hr.at[6], fold_nw, lat)
    fold_to_ne = remote(top_tile, corner.at[3], hs.at[7], hr.at[7], fold_ne, lat)
    own_nw = pltpu.make_async_copy(top_tile, corner.at[2], hr.at[6])
    own_ne = pltpu.make_async_copy(top_tile, corner.at[3], hr.at[7])

    to_west.start()
    to_east.start()

    @pl.when(top)
    def _():
        over_fold.start()

        @pl.when(jnp.logical_not(nw_self))
        def _():
            fold_to_nw.start()

        @pl.when(nw_self)
        def _():
            own_nw.start()

        @pl.when(jnp.logical_not(ne_self))
        def _():
            fold_to_ne.start()

        @pl.when(ne_self)
        def _():
            own_ne.start()

    @pl.when(jnp.logical_not(top))
    def _():
        to_north.start()
        to_nw.start()
        to_ne.start()

    @pl.when(jnp.logical_not(low))
    def _():
        to_south.start()
        to_sw.start()
        to_se.start()

    scale = scale_ref[...]
    scale = jnp.concatenate([scale, scale], axis=0)
    stiff = scale * float(128 * 128)
    root_term = jnp.sqrt(1.0 + 4.0 * stiff)
    log_root = jnp.log1p(-(root_term - 1.0) / (2.0 * stiff))
    gain = (1.0 / root_term) * (2.0 * jnp.sqrt(jnp.sqrt(stiff)))
    both = jnp.where(sub8 < 4, log_root, gain)
    columns = jnp.concatenate([both] * 16, axis=0).T
    place = iota((128, 128), 1).astype(F32) - 63.5
    for block in range(4):
        rows = pl.ds(block * 128, 128)
        power = jnp.broadcast_to(columns[:, block : block + 1], (128, 128)) * place
        gain_rows = jnp.broadcast_to(columns[:, block + 4 : block + 5], (128, 128))
        up = jnp.exp(power)
        down = jnp.exp(-power)
        powers[rows, 0:128] = down
        powers[rows, 128:256] = up
        gains[rows, 0:128] = gain_rows * up
        gains[rows, 128:256] = gain_rows * down
    log_block = log_root * 128.0
    block_decay = jnp.exp(log_block)
    group_decay = jnp.exp(log_block * float(XG))
    image_sum = 1.0 - jnp.exp(log_block * float(nlon))

    def zero_delta(step, carry):
        rows = pl.ds(pl.multiple_of(8 + step * RH, 8), RH)
        delta[0, rows] = jnp.zeros((RH, 128), F32)
        delta[1, rows] = jnp.zeros((RH, 128), F32)
        return carry

    lax.fori_loop(0, 528 // RH, zero_delta, 0)

    first_half = lax.rem(lane8, 16) < 8
    to_east.wait_recv()
    to_west.wait_recv()

    def unturn(step, carry):
        rows = pl.ds(pl.multiple_of(step * 128, 128), 128)
        own = pl.ds(pl.multiple_of(step * 128 + PAD, 16), 128)
        edges = strip_in[:, :, :, rows].reshape(128, 128).T
        for field in range(FIELDS):
            halo[field, own] = roll(edges, -16 * (field + 1), 1)
        return carry

    lax.fori_loop(0, 4, unturn, 0)

    @pl.when(jnp.logical_not(low))
    def _():
        to_north.wait_recv()
        to_nw.wait_recv()
        to_ne.wait_recv()

    south_corner = jnp.where(first_half, corner[1], corner[0])
    for field in range(FIELDS):
        halo[field, pl.ds(8, 8)] = roll(south_corner, -16 * (field + 1), 1)
    to_south.wait_recv()
    to_sw.wait_recv()
    to_se.wait_recv()

    @pl.when(top)
    def _():
        over_fold.wait_send()

    @pl.when(jnp.logical_not(top))
    def _():
        to_north.wait_send()

    @pl.when(jnp.logical_not(low))
    def _():
        to_south.wait_send()

    @pl.when(jnp.logical_not(top))
    def _():
        north_corner = jnp.where(first_half, corner[3], corner[2])
        for field in range(FIELDS):
            halo[field, pl.ds(PAD + 512, 8)] = roll(north_corner, -16 * (field + 1), 1)

    @pl.when(top)
    def _():
        mixed = jnp.where(first_half, corner[2], corner[3])
        tiles = [main[field, pl.ds(PAD + 512, 8)] for field in range(FIELDS)] + [mixed, zero8]
        stack = jnp.concatenate(tiles, axis=0)
        flip = (iota((128, 128), 0) + iota((128, 128), 1) == 127).astype(F32)
        row_to = iota((64, 64), 0)
        row_from = iota((64, 64), 1)
        swap = (row_to // 8 == row_from // 8) & (row_to % 8 + row_from % 8 == 7)
        turned = jnp.dot(stack, flip, precision=HIGH, preferred_element_type=F32)
        turned = jnp.dot(swap.astype(F32), turned, precision=HIGH, preferred_element_type=F32)
        ghost = pl.ds(PAD + 512, 8)
        for field in range(FIELDS):
            inner = turned[8 * field : 8 * field + 8]
            outer = roll(turned[48:56], 16 * (field + 1), 1)
            if field == 2:
                inner, outer = roll(inner, -1, 1), roll(outer, -1, 1)
                inner, outer = (
                    jnp.where(lane8 == 127, outer, inner),
                    jnp.where(lane8 == 127, inner, outer),
                )
            if field == 3:
                last = pl.ds(PAD + 504, 8)
                main[3, last] = jnp.where(sub8 == 7, main[3, last] * inner[0:1], main[3, last])
                halo[3, last] = jnp.where(sub8 == 7, halo[3, last] * outer[0:1], halo[3, last])
                inner, outer = roll(inner, -1, 0), roll(outer, -1, 0)
            main[field, ghost] = inner
            halo[field, ghost] = outer

    last_lane = iota((RH, 128), 1) == 127
    zero_lane = iota((RH, 128), 1) == 0

    def substep(src, dst):
        def rows_of(step, carry):
            row = pl.multiple_of(8 + step * RH, 8)
            here = pl.ds(row, RH)
            wide = pl.ds(row - 8, RH + 16)

            def meridional(state, field):
                values = state[wide]
                face = field[3, wide]
                flux = face * (roll(values, -1, 0) - values)
                return (flux - roll(flux, 1, 0))[8 : RH + 8]

            s_in, s_out = src[0][here], src[1][here]
            e_in, e_out = roll(s_in, -1, 1), roll(s_out, -1, 1)
            f_in = main[2, here] * (jnp.where(last_lane, e_out, e_in) - s_in)
            f_out = halo[2, here] * (jnp.where(last_lane, e_in, e_out) - s_out)
            w_in, w_out = roll(f_in, 1, 1), roll(f_out, 1, 1)
            l_in = f_in - jnp.where(zero_lane, w_out, w_in) + meridional(src[0], main)
            l_out = f_out - jnp.where(zero_lane, w_in, w_out) + meridional(src[1], halo)
            d_in = delta[0, here] + main[1, here] * l_in
            d_out = delta[1, here] + halo[1, here] * l_out
            delta[0, here] = d_in
            delta[1, here] = d_out
            dst[0][here] = s_in + d_in
            dst[1][here] = s_out + d_out
            return carry

        lax.fori_loop(0, 528 // RH, rows_of, 0)

    side_a = (main.at[0], halo.at[0])
    side_b = (work.at[0], work.at[1])

    def forward_pair(step, carry):
        substep(side_a, side_b)
        substep(side_b, side_a)
        return carry

    lax.fori_loop(0, SUBSTEPS // 2, forward_pair, 0)

    def misfit(step, carry):
        here = pl.ds(pl.multiple_of(8 + step * RH, 8), RH)
        for side, field in enumerate((main, halo)):
            start = field[1, here] * field[4, here] * (field[0, here] - field[5, here])
            work[side, here] = start
            delta[side, here] = start
        return carry

    lax.fori_loop(0, 528 // RH, misfit, 0)
    eta_buf[...] = main[0, pl.ds(PAD, 512)]
    eta_out = pltpu.make_async_copy(eta_buf, eta_hbm, out_sem.at[0])
    eta_out.start()

    def adjoint_pair(step, carry):
        substep(side_b, side_a)
        substep(side_a, side_b)
        return carry

    lax.fori_loop(0, SUBSTEPS // 2, adjoint_pair, 0)

    ends = jnp.zeros((8, 128), F32)
    pick_row = iota((8, 256), 0)
    pick_half = 4 * (iota((8, 256), 1) // 128)
    for block in range(4):
        rows = pl.ds(block * 128, 128)
        gradient = delta[0, pl.ds(PAD + block * 128, 128)] / raw_f[0, rows]
        both_ways = jnp.concatenate(
            [gradient * powers[rows, 0:128], gradient * powers[rows, 128:256]], axis=1
        )
        pick = (pick_row == pick_half + block).astype(BF16)
        for index, part in enumerate(split3(both_ways)):
            parts[index, rows] = part
            ends = ends + lax.dot_general(
                pick, part, (((1,), (1,)), ((), ())), preferred_element_type=F32
            )

    xbuf[0] = ends
    x_copies = [
        remote(xbuf.at[0], xbuf.at[step], xs.at[step - 1], xr.at[step - 1], x_peer(step), lat)
        for step in range(1, XG)
    ]
    for copy in x_copies:
        copy.start()

    def local_sums(block, carry):
        col = iota((256, 256), 1)
        row = iota((256, 256), 0)
        ahead = ((row < 128) & (col < 128) & (row <= col)) | (
            (row >= 128) & (col >= 128) & (row > col)
        )
        ahead = ahead.astype(F32).astype(BF16)
        rows = pl.ds(pl.multiple_of(block * 128, 128), 128)
        total = jnp.dot(parts[0, rows], ahead, preferred_element_type=F32)
        total = total + jnp.dot(parts[1, rows], ahead, preferred_element_type=F32)
        total = total + jnp.dot(parts[2, rows], ahead, preferred_element_type=F32)
        sums[rows] = total
        return carry

    forward_half = sub8 < 4
    for copy in x_copies:
        copy.wait_recv()
    group = jnp.zeros((8, 128), F32)
    inside = jnp.zeros((8, 128), F32)
    for step in range(XG):
        source = lax.rem(x_pos + XG - step, XG)
        tile = xbuf[step]
        to_end = jnp.where(forward_half, XG - 1 - source, source).astype(F32)
        group = group + jnp.exp(log_block * to_end) * tile
        ahead = jnp.where(forward_half, x_pos - source, source - x_pos)
        reach = jnp.exp(log_block * jnp.maximum(ahead - 1, 0).astype(F32))
        inside = inside + jnp.where(ahead > 0, reach * tile, 0.0)
    zbuf[0] = group
    z_copies = [
        remote(zbuf.at[0], zbuf.at[step], zs.at[step - 1], zr.at[step - 1], z_peer(step), lat)
        for step in range(1, nz)
    ]
    for copy in z_copies:
        copy.start()

    lax.fori_loop(0, 4, local_sums, 0)

    for copy in z_copies:
        copy.wait_recv()
    inflow = zbuf[0]
    for step in range(nz - 1, 0, -1):
        inflow = inflow * group_decay + jnp.where(forward_half, zbuf[step], zbuf[nz - step])
    steps_in = jnp.where(forward_half, x_pos, XG - 1 - x_pos).astype(F32)
    inflow = inside + jnp.exp(log_block * steps_in) * (inflow / image_sum)
    inflow = inflow * block_decay
    inflow_cols = jnp.concatenate([inflow] * 16, axis=0).T
    for block in range(4):
        rows = pl.ds(block * 128, 128)
        east_in = jnp.broadcast_to(inflow_cols[:, block : block + 1], (128, 128))
        west_in = jnp.broadcast_to(inflow_cols[:, block + 4 : block + 5], (128, 128))
        grad_buf[rows] = gains[rows, 0:128] * (sums[rows, 0:128] + east_in) + gains[
            rows, 128:256
        ] * (sums[rows, 128:256] + west_in)
    grad_out = pltpu.make_async_copy(grad_buf, grad_hbm, out_sem.at[1])
    grad_out.start()

    to_west.wait_send()
    to_east.wait_send()

    @pl.when(top)
    def _():
        @pl.when(jnp.logical_not(nw_self))
        def _():
            fold_to_nw.wait_send()

        @pl.when(jnp.logical_not(ne_self))
        def _():
            fold_to_ne.wait_send()

    @pl.when(jnp.logical_not(top))
    def _():
        to_nw.wait_send()
        to_ne.wait_send()

    @pl.when(jnp.logical_not(low))
    def _():
        to_sw.wait_send()
        to_se.wait_send()

    for copy in x_copies:
        copy.wait_send()
    for copy in z_copies:
        copy.wait_send()
    eta_out.wait()
    grad_out.wait()


def local(
    wet_mask, east_level, north_level, courant, increment, innovation, obs_weight, smooth_scale
):
    nlon = lax.axis_size("lon")
    nlat = lax.axis_size("lat")
    nz = nlon // XG
    any_space = pl.BlockSpec(memory_space=pl.ANY)
    dma = pltpu.SemaphoreType.DMA
    block = jax.ShapeDtypeStruct((512, 128), F32)
    return pl.pallas_call(
        functools.partial(kernel, nlon, nlat),
        out_shape=(block, block),
        in_specs=[any_space] * 7 + [pl.BlockSpec(memory_space=pltpu.VMEM)],
        out_specs=(any_space, any_space),
        scratch_shapes=[
            pltpu.VMEM((3, 512, 128), jnp.int32),
            pltpu.VMEM((2, 512, 128), F32),
            pltpu.VMEM((FIELDS, 544, 128), F32),
            pltpu.VMEM((FIELDS, 544, 128), F32),
            pltpu.VMEM((2, 544, 128), F32),
            pltpu.VMEM((2, 544, 128), F32),
            pltpu.VMEM((512, 128), F32),
            pltpu.VMEM((8, 2, 8, 512), F32),
            pltpu.VMEM((8, 2, 8, 512), F32),
            pltpu.VMEM((4, 8, 128), F32),
            pltpu.VMEM((512, 128), F32),
            pltpu.VMEM((512, 128), F32),
            pltpu.VMEM((512, 256), F32),
            pltpu.VMEM((512, 256), F32),
            pltpu.VMEM((3, 512, 256), BF16),
            pltpu.VMEM((512, 256), F32),
            pltpu.VMEM((XG, 8, 128), F32),
            pltpu.VMEM((nz, 8, 128), F32),
            dma((7,)),
            dma((2,)),
            dma((8,)),
            dma((8,)),
            dma((XG - 1,)),
            dma((XG - 1,)),
            dma((nz - 1,)),
            dma((nz - 1,)),
        ],
        compiler_params=pltpu.CompilerParams(
            collective_id=0, has_side_effects=True, vmem_limit_bytes=32 * 1024 * 1024
        ),
    )(
        wet_mask,
        east_level,
        north_level,
        courant,
        increment,
        innovation,
        obs_weight,
        smooth_scale.reshape(4, 128),
    )


def solution(mesh):
    return jax.shard_map(
        local,
        mesh=mesh,
        in_specs=(P("lat", "lon"),) * 7 + (P("lat"),),
        out_specs=(P("lat", "lon"), P("lat", "lon")),
        check_vma=False,
    )
```

time: 886 us -> 59.3 us (0.07)
  the two profiles are of different devices: /device:TPU:2 before, /device:TPU:26 now
where the time goes in v1:
time: 59.3 us; the launch traced here: 58.9 us
  Pallas kernels  49.6 us (84%)
  local copies, waits for them, and re-layouts  8.73 us (15%)
  between operations  0.66 us (1%)
    pallas_call x1, Pallas kernels, local(): pl.pallas_call(functools.partial(kernel, nlon, nlat), out_shape=(block, b...  49.6 us
    unnamed x18, local copies, waits for them, and re-layouts  8.73 us

profile of v1, /device:TPU:26, one launch (start us, length us, event | category | flops | bytes accessed | tf_op | source)
XLA Modules:
  0.0 58.9 jit_solution(17948758515027529075)
XLA Ops:
  0.6 0.0 copy-start
  0.6 0.9 %copy-done = s32[512,128]{1,0:T(8,128)S(1)} copy-done((s32[512,128]{1,0:T(8,128)S(1)}, s32[512,128]{1,0:T(8,128)}, u32[]{:S(2)}) %copy-start) | copy-done | bytes 262168
  1.6 0.0 copy-start.1
  1.6 0.9 %copy-done.1 = s32[512,128]{1,0:T(8,128)S(1)} copy-done((s32[512,128]{1,0:T(8,128)S(1)}, s32[512,128]{1,0:T(8,128)}, u32[]{:S(2)}) %copy-start.1) | copy-done | bytes 262168
  2.5 0.0 copy-start.2
  2.5 0.9 %copy-done.2 = s32[512,128]{1,0:T(8,128)S(1)} copy-done((s32[512,128]{1,0:T(8,128)S(1)}, s32[512,128]{1,0:T(8,128)}, u32[]{:S(2)}) %copy-start.2) | copy-done | bytes 262168
  3.5 0.0 copy-start.3
  3.5 0.9 %copy-done.3 = f32[512,128]{1,0:T(8,128)S(1)} copy-done((f32[512,128]{1,0:T(8,128)S(1)}, f32[512,128]{1,0:T(8,128)}, u32[]{:S(2)}) %copy-start.3) | copy-done | bytes 262168
  4.4 0.0 copy-start.4
  4.4 0.9 %copy-done.4 = f32[512,128]{1,0:T(8,128)S(1)} copy-done((f32[512,128]{1,0:T(8,128)S(1)}, f32[512,128]{1,0:T(8,128)}, u32[]{:S(2)}) %copy-start.4) | copy-done | bytes 262168
  5.4 0.0 copy-start.5
  5.4 0.9 %copy-done.5 = f32[512,128]{1,0:T(8,128)S(1)} copy-done((f32[512,128]{1,0:T(8,128)S(1)}, f32[512,128]{1,0:T(8,128)}, u32[]{:S(2)}) %copy-start.5) | copy-done | bytes 262168
  6.3 0.0 copy-start.6
  6.3 0.9 %copy-done.6 = f32[512,128]{1,0:T(8,128)S(1)} copy-done((f32[512,128]{1,0:T(8,128)S(1)}, f32[512,128]{1,0:T(8,128)}, u32[]{:S(2)}) %copy-start.6) | copy-done | bytes 262168
  7.3 0.0 copy-start.7
  7.3 0.7 %copy-done.7 = f32[512]{0:T(512)S(1)} copy-done((f32[512]{0:T(512)S(1)}, f32[512]{0:T(512)}, u32[]{:S(2)}) %copy-start.7) | copy-done | bytes 2072
  8.0 49.6 %shard_map.95 = (f32[512,128]{1,0:T(8,128)S(1)}, f32[512,128]{1,0:T(8,128)S(1)}) custom-call(s32[512,128]{1,0:T(8,128)S(1)} %copy-done, s32[512,128]{1,0:T(8,128)S(1)} %copy-done.1, s32[512,128]{1,0:T(8,128)S(1)} %copy-done.2, f32[512,128]{1,0:T(8,128)S(1)} %copy-done.3, f32[512,128]{1,0:T(8,128)S(1)} %copy-done.4, f32[512,128]{1,0:T(8,128)S(1)} %copy-done.5, ...), custom_call_target="tpu_custom_call" | custom-call | tf_op jit(solution)/shard_map/pallas_call | solution.py:573
  57.5 0.7 %copy.12 = f32[512,128]{1,0:T(8,128)} copy(f32[512,128]{1,0:T(8,128)S(1)} %get-tuple-element.4) | data formatting | bytes 524288
  58.2 0.7 %copy.13 = f32[512,128]{1,0:T(8,128)} copy(f32[512,128]{1,0:T(8,128)S(1)} %get-tuple-element.5) | data formatting | bytes 524288
Async XLA Ops:
  0.6 1.0 %copy-start = (s32[512,128]{1,0:T(8,128)S(1)}, s32[512,128]{1,0:T(8,128)}, u32[]{:S(2)}) copy-start(s32[512,128]{1,0:T(8,128)} %wet_hbm.1) | copy-start | bytes 786436
  1.6 0.9 %copy-start.1 = (s32[512,128]{1,0:T(8,128)S(1)}, s32[512,128]{1,0:T(8,128)}, u32[]{:S(2)}) copy-start(s32[512,128]{1,0:T(8,128)} %east_hbm.1) | copy-start | bytes 786436
  2.5 0.9 %copy-start.2 = (s32[512,128]{1,0:T(8,128)S(1)}, s32[512,128]{1,0:T(8,128)}, u32[]{:S(2)}) copy-start(s32[512,128]{1,0:T(8,128)} %north_hbm.1) | copy-start | bytes 786436
  3.5 0.9 %copy-start.3 = (f32[512,128]{1,0:T(8,128)S(1)}, f32[512,128]{1,0:T(8,128)}, u32[]{:S(2)}) copy-start(f32[512,128]{1,0:T(8,128)} %cour_hbm.1) | copy-start | bytes 786436
  4.4 0.9 %copy-start.4 = (f32[512,128]{1,0:T(8,128)S(1)}, f32[512,128]{1,0:T(8,128)}, u32[]{:S(2)}) copy-start(f32[512,128]{1,0:T(8,128)} %incr_hbm.1) | copy-start | bytes 786436
  5.4 0.9 %copy-start.5 = (f32[512,128]{1,0:T(8,128)S(1)}, f32[512,128]{1,0:T(8,128)}, u32[]{:S(2)}) copy-start(f32[512,128]{1,0:T(8,128)} %innov_hbm.1) | copy-start | bytes 786436
  6.3 0.9 %copy-start.6 = (f32[512,128]{1,0:T(8,128)S(1)}, f32[512,128]{1,0:T(8,128)}, u32[]{:S(2)}) copy-start(f32[512,128]{1,0:T(8,128)} %ow_hbm.1) | copy-start | bytes 786436
  7.3 0.7 %copy-start.7 = (f32[512]{0:T(512)S(1)}, f32[512]{0:T(512)}, u32[]{:S(2)}) copy-start(f32[512]{0:T(512)} %param.15) | copy-start | bytes 6148

commit v2 on v1

--- a/solution.py
+++ b/solution.py
@@ -12,8 +12,9 @@
 BF16 = jnp.bfloat16
 XG = 4
 FIELDS = 6
+WEST = 6
 PAD = 16
-RH = 48
+RH = 24
 HIGH = lax.Precision.HIGHEST
 
 
@@ -54,9 +55,9 @@
     incr_hbm,
     innov_hbm,
     ow_hbm,
-    scale_ref,
-    eta_hbm,
-    grad_hbm,
+    scale_hbm,
+    eta_ref,
+    grad_ref,
     raw_i,
     raw_f,
     main,
@@ -67,8 +68,7 @@
     strip_out,
     strip_in,
     corner,
-    eta_buf,
-    grad_buf,
+    scale_buf,
     powers,
     gains,
     parts,
@@ -76,7 +76,6 @@
     xbuf,
     zbuf,
     in_sem,
-    out_sem,
     hs,
     hr,
     xs,
@@ -100,6 +99,7 @@
     nw_self = fold_nw == lon
 
     loads = [
+        pltpu.make_async_copy(scale_hbm, scale_buf, in_sem.at[7]),
         pltpu.make_async_copy(wet_hbm, raw_i.at[0], in_sem.at[0]),
         pltpu.make_async_copy(cour_hbm, raw_f.at[0], in_sem.at[1]),
         pltpu.make_async_copy(incr_hbm, raw_f.at[1], in_sem.at[2]),
@@ -184,37 +184,29 @@
 
     for load in loads:
         load.wait()
-    slot = (iota((64, 128), 1) + 8) // 16
-
-    def build(step, carry):
-        row = pl.multiple_of(step * 64, 64)
-        own = pl.ds(pl.multiple_of(step * 64 + PAD, 16), 64)
-        rows = pl.ds(row, 64)
-        wet = raw_i[0, rows].astype(F32)
-        fields = [
-            wet * raw_f[1, rows],
-            wet * raw_f[0, rows],
-            raw_i[1, rows].astype(F32) * (1.0 / WLEV),
-            raw_i[2, rows].astype(F32) * (1.0 / WLEV),
-        ]
-        for index, value in enumerate(fields):
-            main[index, own] = value
-        fields.append(main[4, own])
-        fields.append(main[5, own])
-        joined = roll(fields[0], 16, 1)
-        for index in range(1, FIELDS):
-            joined = jnp.where(slot == index + 1, roll(fields[index], 16 * (index + 1), 1), joined)
-        packed[rows] = joined
-        return carry
-
-    lax.fori_loop(0, 8, build, 0)
-
-    def turn(step, carry):
-        rows = pl.ds(pl.multiple_of(step * 128, 128), 128)
+    slot = (iota((32, 128), 1) + 8) // 16
+    for block in range(4):
+        for row in range(128 * block, 128 * block + 128, 32):
+            rows, own = pl.ds(row, 32), pl.ds(row + PAD, 32)
+            wet = raw_i[0, rows].astype(F32)
+            fields = [
+                wet * raw_f[1, rows],
+                wet * raw_f[0, rows],
+                raw_i[1, rows].astype(F32) * (1.0 / WLEV),
+                raw_i[2, rows].astype(F32) * (1.0 / WLEV),
+            ]
+            for index, value in enumerate(fields):
+                main[index, own] = value
+            main[WEST, own] = roll(fields[2], 1, 1)
+            fields.append(main[4, own])
+            fields.append(main[5, own])
+            joined = roll(fields[0], 16, 1)
+            for index in range(1, FIELDS):
+                moved = roll(fields[index], 16 * (index + 1), 1)
+                joined = jnp.where(slot == index + 1, moved, joined)
+            packed[rows] = joined
+        rows = pl.ds(128 * block, 128)
         strip_out[:, :, :, rows] = packed[rows].T.reshape(8, 2, 8, 128)
-        return carry
-
-    lax.fori_loop(0, 4, turn, 0)
 
     links = 2 + (XG - 1) + (nz - 1)
     north_links = jnp.where(
@@ -223,10 +215,10 @@
     south_links = jnp.where(low, 0, 3)
     pl.semaphore_wait(barrier, links + north_links + south_links)
 
-    top_rows = main.at[:, pl.ds(PAD + 504, 8)]
-    low_rows = main.at[:, pl.ds(PAD, 8)]
-    south_halo = main.at[:, pl.ds(8, 8)]
-    north_halo = main.at[:, pl.ds(PAD + 512, 8)]
+    top_rows = main.at[pl.ds(0, FIELDS), pl.ds(PAD + 504, 8)]
+    low_rows = main.at[pl.ds(0, FIELDS), pl.ds(PAD, 8)]
+    south_halo = main.at[pl.ds(0, FIELDS), pl.ds(8, 8)]
+    north_halo = main.at[pl.ds(0, FIELDS), pl.ds(PAD + 512, 8)]
     top_tile = packed.at[pl.ds(504, 8)]
     low_tile = packed.at[pl.ds(0, 8)]
     to_west = remote(
@@ -282,7 +274,7 @@
         to_sw.start()
         to_se.start()
 
-    scale = scale_ref[...]
+    scale = scale_buf[...]
     scale = jnp.concatenate([scale, scale], axis=0)
     stiff = scale * float(128 * 128)
     root_term = jnp.sqrt(1.0 + 4.0 * stiff)
@@ -306,27 +298,26 @@
     group_decay = jnp.exp(log_block * float(XG))
     image_sum = 1.0 - jnp.exp(log_block * float(nlon))
 
-    def zero_delta(step, carry):
-        rows = pl.ds(pl.multiple_of(8 + step * RH, 8), RH)
-        delta[0, rows] = jnp.zeros((RH, 128), F32)
-        delta[1, rows] = jnp.zeros((RH, 128), F32)
-        return carry
-
-    lax.fori_loop(0, 528 // RH, zero_delta, 0)
+    for row in range(8, 536, RH):
+        delta[0, pl.ds(row, RH)] = jnp.zeros((RH, 128), F32)
+        delta[1, pl.ds(row, RH)] = jnp.zeros((RH, 128), F32)
 
     first_half = lax.rem(lane8, 16) < 8
     to_east.wait_recv()
     to_west.wait_recv()
 
-    def unturn(step, carry):
-        rows = pl.ds(pl.multiple_of(step * 128, 128), 128)
-        own = pl.ds(pl.multiple_of(step * 128 + PAD, 16), 128)
-        edges = strip_in[:, :, :, rows].reshape(128, 128).T
+    def set_west(rows, outer):
+        inner = main[WEST, rows]
+        first = iota(inner.shape, 1) == 0
+        main[WEST, rows] = jnp.where(first, outer, inner)
+        halo[WEST, rows] = jnp.where(first, inner, outer)
+
+    for block in range(4):
+        own = pl.ds(128 * block + PAD, 128)
+        edges = strip_in[:, :, :, pl.ds(128 * block, 128)].reshape(128, 128).T
         for field in range(FIELDS):
             halo[field, own] = roll(edges, -16 * (field + 1), 1)
-        return carry
-
-    lax.fori_loop(0, 4, unturn, 0)
+        set_west(own, roll(edges, 1 - 16 * 3, 1))
 
     @pl.when(jnp.logical_not(low))
     def _():
@@ -388,37 +379,30 @@
             main[field, ghost] = inner
             halo[field, ghost] = outer
 
+    for edge in (8, PAD + 512):
+        rows = pl.ds(edge, 8)
+        main[WEST, rows] = roll(main[2, rows], 1, 1)
+        set_west(rows, roll(halo[2, rows], 1, 1))
+
     last_lane = iota((RH, 128), 1) == 127
     zero_lane = iota((RH, 128), 1) == 0
 
     def substep(src, dst):
-        def rows_of(step, carry):
-            row = pl.multiple_of(8 + step * RH, 8)
-            here = pl.ds(row, RH)
-            wide = pl.ds(row - 8, RH + 16)
-
-            def meridional(state, field):
-                values = state[wide]
-                face = field[3, wide]
-                flux = face * (roll(values, -1, 0) - values)
-                return (flux - roll(flux, 1, 0))[8 : RH + 8]
-
-            s_in, s_out = src[0][here], src[1][here]
-            e_in, e_out = roll(s_in, -1, 1), roll(s_out, -1, 1)
-            f_in = main[2, here] * (jnp.where(last_lane, e_out, e_in) - s_in)
-            f_out = halo[2, here] * (jnp.where(last_lane, e_in, e_out) - s_out)
-            w_in, w_out = roll(f_in, 1, 1), roll(f_out, 1, 1)
-            l_in = f_in - jnp.where(zero_lane, w_out, w_in) + meridional(src[0], main)
-            l_out = f_out - jnp.where(zero_lane, w_in, w_out) + meridional(src[1], halo)
-            d_in = delta[0, here] + main[1, here] * l_in
-            d_out = delta[1, here] + halo[1, here] * l_out
-            delta[0, here] = d_in
-            delta[1, here] = d_out
-            dst[0][here] = s_in + d_in
-            dst[1][here] = s_out + d_out
-            return carry
-
-        lax.fori_loop(0, 528 // RH, rows_of, 0)
+        for row in range(8, 536, RH):
+            here, up, down = pl.ds(row, RH), pl.ds(row + 1, RH), pl.ds(row - 1, RH)
+            states = [src[side][here] for side in range(2)]
+            east = [roll(state, -1, 1) for state in states]
+            west = [roll(state, 1, 1) for state in states]
+            for side, field in enumerate((main, halo)):
+                state = states[side]
+                to_east = jnp.where(last_lane, east[1 - side], east[side]) - state
+                to_west = jnp.where(zero_lane, west[1 - side], west[side]) - state
+                spread = field[2, here] * to_east + field[WEST, here] * to_west
+                spread = spread + field[3, here] * (src[side][up] - state)
+                spread = spread + field[3, down] * (src[side][down] - state)
+                change = delta[side, here] + field[1, here] * spread
+                delta[side, here] = change
+                dst[side][here] = state + change
 
     side_a = (main.at[0], halo.at[0])
     side_b = (work.at[0], work.at[1])
@@ -430,18 +414,13 @@
 
     lax.fori_loop(0, SUBSTEPS // 2, forward_pair, 0)
 
-    def misfit(step, carry):
-        here = pl.ds(pl.multiple_of(8 + step * RH, 8), RH)
+    for row in range(8, 536, RH):
+        here = pl.ds(row, RH)
         for side, field in enumerate((main, halo)):
             start = field[1, here] * field[4, here] * (field[0, here] - field[5, here])
             work[side, here] = start
             delta[side, here] = start
-        return carry
-
-    lax.fori_loop(0, 528 // RH, misfit, 0)
-    eta_buf[...] = main[0, pl.ds(PAD, 512)]
-    eta_out = pltpu.make_async_copy(eta_buf, eta_hbm, out_sem.at[0])
-    eta_out.start()
+    eta_ref[...] = main[0, pl.ds(PAD, 512)]
 
     def adjoint_pair(step, carry):
         substep(side_b, side_a)
@@ -469,24 +448,10 @@
     xbuf[0] = ends
     x_copies = [
         remote(xbuf.at[0], xbuf.at[step], xs.at[step - 1], xr.at[step - 1], x_peer(step), lat)
-        for step in range(1, XG)
+        for step in (2, 1, 3)
     ]
     for copy in x_copies:
         copy.start()
-
-    def local_sums(block, carry):
-        col = iota((256, 256), 1)
-        row = iota((256, 256), 0)
-        ahead = ((row < 128) & (col < 128) & (row <= col)) | (
-            (row >= 128) & (col >= 128) & (row > col)
-        )
-        ahead = ahead.astype(F32).astype(BF16)
-        rows = pl.ds(pl.multiple_of(block * 128, 128), 128)
-        total = jnp.dot(parts[0, rows], ahead, preferred_element_type=F32)
-        total = total + jnp.dot(parts[1, rows], ahead, preferred_element_type=F32)
-        total = total + jnp.dot(parts[2, rows], ahead, preferred_element_type=F32)
-        sums[rows] = total
-        return carry
 
     forward_half = sub8 < 4
     for copy in x_copies:
@@ -504,12 +469,20 @@
     zbuf[0] = group
     z_copies = [
         remote(zbuf.at[0], zbuf.at[step], zs.at[step - 1], zr.at[step - 1], z_peer(step), lat)
-        for step in range(1, nz)
+        for step in sorted(range(1, nz), key=lambda step: -min(step, nz - step))
     ]
     for copy in z_copies:
         copy.start()
 
-    lax.fori_loop(0, 4, local_sums, 0)
+    col = iota((256, 256), 1)
+    row = iota((256, 256), 0)
+    ahead = ((row < 128) & (col < 128) & (row <= col)) | ((row >= 128) & (col >= 128) & (row > col))
+    ahead = ahead.astype(F32).astype(BF16)
+    for block in range(4):
+        rows = pl.ds(block * 128, 128)
+        total = jnp.dot(parts[0, rows], ahead, preferred_element_type=F32)
+        total = total + jnp.dot(parts[1, rows], ahead, preferred_element_type=F32)
+        sums[rows] = total + jnp.dot(parts[2, rows], ahead, preferred_element_type=F32)
 
     for copy in z_copies:
         copy.wait_recv()
@@ -524,11 +497,9 @@
         rows = pl.ds(block * 128, 128)
         east_in = jnp.broadcast_to(inflow_cols[:, block : block + 1], (128, 128))
         west_in = jnp.broadcast_to(inflow_cols[:, block + 4 : block + 5], (128, 128))
-        grad_buf[rows] = gains[rows, 0:128] * (sums[rows, 0:128] + east_in) + gains[
+        grad_ref[rows] = gains[rows, 0:128] * (sums[rows, 0:128] + east_in) + gains[
             rows, 128:256
         ] * (sums[rows, 128:256] + west_in)
-    grad_out = pltpu.make_async_copy(grad_buf, grad_hbm, out_sem.at[1])
-    grad_out.start()
 
     to_west.wait_send()
     to_east.wait_send()
@@ -557,8 +528,6 @@
         copy.wait_send()
     for copy in z_copies:
         copy.wait_send()
-    eta_out.wait()
-    grad_out.wait()
 
 
 def local(
@@ -567,35 +536,34 @@
     nlon = lax.axis_size("lon")
     nlat = lax.axis_size("lat")
     nz = nlon // XG
-    any_space = pl.BlockSpec(memory_space=pl.ANY)
+    hbm = pl.BlockSpec(memory_space=pltpu.MemorySpace.HBM)
+    vmem = pl.BlockSpec(memory_space=pltpu.VMEM)
     dma = pltpu.SemaphoreType.DMA
     block = jax.ShapeDtypeStruct((512, 128), F32)
     return pl.pallas_call(
         functools.partial(kernel, nlon, nlat),
         out_shape=(block, block),
-        in_specs=[any_space] * 7 + [pl.BlockSpec(memory_space=pltpu.VMEM)],
-        out_specs=(any_space, any_space),
+        in_specs=[hbm] * 8,
+        out_specs=(vmem, vmem),
         scratch_shapes=[
             pltpu.VMEM((3, 512, 128), jnp.int32),
             pltpu.VMEM((2, 512, 128), F32),
-            pltpu.VMEM((FIELDS, 544, 128), F32),
-            pltpu.VMEM((FIELDS, 544, 128), F32),
+            pltpu.VMEM((FIELDS + 1, 544, 128), F32),
+            pltpu.VMEM((FIELDS + 1, 544, 128), F32),
             pltpu.VMEM((2, 544, 128), F32),
             pltpu.VMEM((2, 544, 128), F32),
             pltpu.VMEM((512, 128), F32),
             pltpu.VMEM((8, 2, 8, 512), F32),
             pltpu.VMEM((8, 2, 8, 512), F32),
             pltpu.VMEM((4, 8, 128), F32),
-            pltpu.VMEM((512, 128), F32),
-            pltpu.VMEM((512, 128), F32),
+            pltpu.VMEM((4, 128), F32),
             pltpu.VMEM((512, 256), F32),
             pltpu.VMEM((512, 256), F32),
             pltpu.VMEM((3, 512, 256), BF16),
             pltpu.VMEM((512, 256), F32),
             pltpu.VMEM((XG, 8, 128), F32),
             pltpu.VMEM((nz, 8, 128), F32),
-            dma((7,)),
-            dma((2,)),
+            dma((8,)),
             dma((8,)),
             dma((8,)),
             dma((XG - 1,)),
@@ -604,7 +572,7 @@
             dma((nz - 1,)),
         ],
         compiler_params=pltpu.CompilerParams(
-            collective_id=0, has_side_effects=True, vmem_limit_bytes=32 * 1024 * 1024
+            collective_id=0, has_side_effects=True, vmem_limit_bytes=54656 * 1024
         ),
     )(
         wet_mask,

time: 59.3 us -> 39.4 us (0.66)
  Pallas kernels: 49.6 us -> 36.5 us
  local copies, waits for them, and re-layouts: 8.73 us -> 2.08 us
    pallas_call x1, Pallas kernels: 49.6 us -> 36.5 us  [local(): pl.pallas_call(functools.partial(kernel, nlon, nlat), out_shape=(block, b...]
    unnamed x18 -> x4, local copies, waits for them, and re-layouts: 8.73 us -> 2.08 us
where the time goes in v2:
time: 39.4 us; the launch traced here: 39.2 us
  Pallas kernels  36.5 us (93%)
  local copies, waits for them, and re-layouts  2.08 us (5%)
  between operations  0.65 us (2%)
    pallas_call x1, Pallas kernels, local(): pl.pallas_call(functools.partial(kernel, nlon, nlat), out_shape=(block, b...  36.5 us
    unnamed x4, local copies, waits for them, and re-layouts  2.08 us

profile of v2, /device:TPU:26, one launch (start us, length us, event | category | flops | bytes accessed | tf_op | source)
XLA Modules:
  0.0 39.2 jit_solution(13116377077985447434)
XLA Ops:
  0.6 0.0 copy-start
  0.6 0.7 %copy-done = f32[512]{0:T(512)S(1)} copy-done((f32[512]{0:T(512)S(1)}, f32[512]{0:T(512)}, u32[]{:S(2)}) %copy-start) | copy-done | bytes 2072
  1.3 36.5 %shard_map.95 = (f32[512,128]{1,0:T(8,128)S(1)}, f32[512,128]{1,0:T(8,128)S(1)}) custom-call(s32[512,128]{1,0:T(8,128)} %wet_hbm.1, s32[512,128]{1,0:T(8,128)} %east_hbm.1, s32[512,128]{1,0:T(8,128)} %north_hbm.1, f32[512,128]{1,0:T(8,128)} %cour_hbm.1, f32[512,128]{1,0:T(8,128)} %incr_hbm.1, f32[512,128]{1,0:T(8,128)} %innov_hbm.1, f32[512,128]{1,0:T(8,128)} %ow_hbm.1, ...), custom_call_target="tpu_custom_call" | custom-call | tf_op jit(solution)/shard_map/pallas_call | solution.py:543
  37.8 0.7 %copy.12 = f32[512,128]{1,0:T(8,128)} copy(f32[512,128]{1,0:T(8,128)S(1)} %get-tuple-element.4) | data formatting | bytes 524288
  38.5 0.7 %copy.13 = f32[512,128]{1,0:T(8,128)} copy(f32[512,128]{1,0:T(8,128)S(1)} %get-tuple-element.5) | data formatting | bytes 524288
Async XLA Ops:
  0.6 0.7 %copy-start = (f32[512]{0:T(512)S(1)}, f32[512]{0:T(512)}, u32[]{:S(2)}) copy-start(f32[512]{0:T(512)} %param.15) | copy-start | bytes 6148

commit v3 on v2

--- a/solution.py
+++ b/solution.py
@@ -75,6 +75,7 @@
     sums,
     xbuf,
     zbuf,
+    z_weight,
     in_sem,
     hs,
     hr,
@@ -108,9 +109,6 @@
         pltpu.make_async_copy(ow_hbm, main.at[4, pl.ds(PAD, 512)], in_sem.at[5]),
         pltpu.make_async_copy(innov_hbm, main.at[5, pl.ds(PAD, 512)], in_sem.at[6]),
     ]
-    for load in loads:
-        load.start()
-
     barrier = pltpu.get_barrier_semaphore()
 
     def greet(to_lon, to_lat):
@@ -154,20 +152,21 @@
         def _():
             greet(fold_nw, lat)
 
+    for load in loads:
+        load.start()
+    far_first = sorted(range(1, nz), key=lambda step: -min(step, nz - step))
+    for step in far_first:
+        greet(z_peer(step), lat)
     for step in range(1, XG):
         greet(x_peer(step), lat)
-    for step in range(1, nz):
-        greet(z_peer(step), lat)
 
     lane8 = iota((8, 128), 1)
     sub8 = iota((8, 128), 0)
 
     zero8 = jnp.zeros((8, 128), F32)
-    zstrip = jnp.zeros((8, 512), F32)
-    strip_in[0, 0] = zstrip
-    strip_in[6, 1] = zstrip
-    strip_in[7, 0] = zstrip
-    strip_in[7, 1] = zstrip
+    for block in range(4):
+        for slot, side in ((0, 0), (6, 1), (7, 0), (7, 1)):
+            strip_in[block, slot, side] = zero8
     for edge in (0, 536):
         for field in (0, 3):
             main[field, pl.ds(edge, 8)] = zero8
@@ -205,8 +204,6 @@
                 moved = roll(fields[index], 16 * (index + 1), 1)
                 joined = jnp.where(slot == index + 1, moved, joined)
             packed[rows] = joined
-        rows = pl.ds(128 * block, 128)
-        strip_out[:, :, :, rows] = packed[rows].T.reshape(8, 2, 8, 128)
 
     links = 2 + (XG - 1) + (nz - 1)
     north_links = jnp.where(
@@ -221,12 +218,12 @@
     north_halo = main.at[pl.ds(0, FIELDS), pl.ds(PAD + 512, 8)]
     top_tile = packed.at[pl.ds(504, 8)]
     low_tile = packed.at[pl.ds(0, 8)]
-    to_west = remote(
-        strip_out.at[pl.ds(1, 6), 0], strip_in.at[pl.ds(1, 6), 0], hs.at[2], hr.at[3], west_lon, lat
-    )
-    to_east = remote(
-        strip_out.at[pl.ds(0, 6), 1], strip_in.at[pl.ds(0, 6), 1], hs.at[3], hr.at[2], east_lon, lat
-    )
+    to_west, to_east = [], []
+    for block in range(4):
+        first = strip_out.at[block, pl.ds(1, 6), 0], strip_in.at[block, pl.ds(1, 6), 0]
+        last = strip_out.at[block, pl.ds(0, 6), 1], strip_in.at[block, pl.ds(0, 6), 1]
+        to_west.append(remote(*first, hs.at[8 + block], hr.at[8 + block], west_lon, lat))
+        to_east.append(remote(*last, hs.at[12 + block], hr.at[12 + block], east_lon, lat))
     to_south = remote(low_rows, north_halo, hs.at[0], hr.at[1], lon, lat - 1)
     to_sw = remote(low_tile, corner.at[3], hs.at[4], hr.at[7], west_lon, lat - 1)
     to_se = remote(low_tile, corner.at[2], hs.at[5], hr.at[6], east_lon, lat - 1)
@@ -239,9 +236,6 @@
     own_nw = pltpu.make_async_copy(top_tile, corner.at[2], hr.at[6])
     own_ne = pltpu.make_async_copy(top_tile, corner.at[3], hr.at[7])
 
-    to_west.start()
-    to_east.start()
-
     @pl.when(top)
     def _():
         over_fold.start()
@@ -273,6 +267,12 @@
         to_south.start()
         to_sw.start()
         to_se.start()
+
+    for block in range(4):
+        turned = packed[pl.ds(128 * block, 128)].T
+        strip_out[block] = turned.reshape(8, 2, 8, 128)
+        to_west[block].start()
+        to_east[block].start()
 
     scale = scale_buf[...]
     scale = jnp.concatenate([scale, scale], axis=0)
@@ -294,7 +294,6 @@
         gains[rows, 0:128] = gain_rows * up
         gains[rows, 128:256] = gain_rows * down
     log_block = log_root * 128.0
-    block_decay = jnp.exp(log_block)
     group_decay = jnp.exp(log_block * float(XG))
     image_sum = 1.0 - jnp.exp(log_block * float(nlon))
 
@@ -303,9 +302,6 @@
         delta[1, pl.ds(row, RH)] = jnp.zeros((RH, 128), F32)
 
     first_half = lax.rem(lane8, 16) < 8
-    to_east.wait_recv()
-    to_west.wait_recv()
-
     def set_west(rows, outer):
         inner = main[WEST, rows]
         first = iota(inner.shape, 1) == 0
@@ -314,7 +310,9 @@
 
     for block in range(4):
         own = pl.ds(128 * block + PAD, 128)
-        edges = strip_in[:, :, :, pl.ds(128 * block, 128)].reshape(128, 128).T
+        to_west[block].wait_recv()
+        to_east[block].wait_recv()
+        edges = strip_in[block].reshape(128, 128).T
         for field in range(FIELDS):
             halo[field, own] = roll(edges, -16 * (field + 1), 1)
         set_west(own, roll(edges, 1 - 16 * 3, 1))
@@ -445,6 +443,20 @@
                 pick, part, (((1,), (1,)), ((), ())), preferred_element_type=F32
             )
 
+    forward_half = sub8 < 4
+    to_end, reach = [], []
+    for step in range(XG):
+        source = lax.rem(x_pos + XG - step, XG)
+        blocks = jnp.where(forward_half, XG - 1 - source, source).astype(F32)
+        to_end.append(jnp.exp(log_block * blocks))
+        ahead = jnp.where(forward_half, x_pos - source, source - x_pos)
+        near = jnp.exp(log_block * jnp.maximum(ahead, 1).astype(F32))
+        reach.append(jnp.where(ahead > 0, near, 0.0))
+    steps_in = jnp.where(forward_half, x_pos, XG - 1 - x_pos).astype(F32)
+    group_weight = jnp.exp(log_block * (steps_in + 1.0)) / image_sum
+    for step in range(1, nz + 1):
+        z_weight[step - 1] = group_weight
+        group_weight = group_weight * group_decay
     xbuf[0] = ends
     x_copies = [
         remote(xbuf.at[0], xbuf.at[step], xs.at[step - 1], xr.at[step - 1], x_peer(step), lat)
@@ -453,23 +465,14 @@
     for copy in x_copies:
         copy.start()
 
-    forward_half = sub8 < 4
     for copy in x_copies:
         copy.wait_recv()
-    group = jnp.zeros((8, 128), F32)
-    inside = jnp.zeros((8, 128), F32)
-    for step in range(XG):
-        source = lax.rem(x_pos + XG - step, XG)
-        tile = xbuf[step]
-        to_end = jnp.where(forward_half, XG - 1 - source, source).astype(F32)
-        group = group + jnp.exp(log_block * to_end) * tile
-        ahead = jnp.where(forward_half, x_pos - source, source - x_pos)
-        reach = jnp.exp(log_block * jnp.maximum(ahead - 1, 0).astype(F32))
-        inside = inside + jnp.where(ahead > 0, reach * tile, 0.0)
+    tiles = [xbuf[step] for step in range(XG)]
+    group = sum(to_end[step] * tiles[step] for step in range(XG))
     zbuf[0] = group
     z_copies = [
         remote(zbuf.at[0], zbuf.at[step], zs.at[step - 1], zr.at[step - 1], z_peer(step), lat)
-        for step in sorted(range(1, nz), key=lambda step: -min(step, nz - step))
+        for step in far_first
     ]
     for copy in z_copies:
         copy.start()
@@ -484,25 +487,32 @@
         total = total + jnp.dot(parts[1, rows], ahead, preferred_element_type=F32)
         sums[rows] = total + jnp.dot(parts[2, rows], ahead, preferred_element_type=F32)
 
+    inside = sum(reach[step] * tiles[step] for step in range(XG))
+    for block in range(4):
+        rows = pl.ds(block * 128, 128)
+        both_gains = gains[rows]
+        both_sums = both_gains * sums[rows]
+        grad_ref[rows] = both_sums[:, 0:128] + both_sums[:, 128:256]
+
     for copy in z_copies:
         copy.wait_recv()
-    inflow = zbuf[0]
-    for step in range(nz - 1, 0, -1):
-        inflow = inflow * group_decay + jnp.where(forward_half, zbuf[step], zbuf[nz - step])
-    steps_in = jnp.where(forward_half, x_pos, XG - 1 - x_pos).astype(F32)
-    inflow = inside + jnp.exp(log_block * steps_in) * (inflow / image_sum)
-    inflow = inflow * block_decay
+    terms = [inside]
+    for step in range(1, nz + 1):
+        tile = jnp.where(forward_half, zbuf[step % nz], zbuf[(nz - step) % nz])
+        terms.append(z_weight[step - 1] * tile)
+    while len(terms) > 1:
+        terms = [a + b for a, b in zip(terms[::2], terms[1::2])] + terms[len(terms) // 2 * 2 :]
+    inflow = terms[0]
     inflow_cols = jnp.concatenate([inflow] * 16, axis=0).T
     for block in range(4):
         rows = pl.ds(block * 128, 128)
         east_in = jnp.broadcast_to(inflow_cols[:, block : block + 1], (128, 128))
         west_in = jnp.broadcast_to(inflow_cols[:, block + 4 : block + 5], (128, 128))
-        grad_ref[rows] = gains[rows, 0:128] * (sums[rows, 0:128] + east_in) + gains[
-            rows, 128:256
-        ] * (sums[rows, 128:256] + west_in)
-
-    to_west.wait_send()
-    to_east.wait_send()
+        inner = gains[rows, 0:128] * east_in + gains[rows, 128:256] * west_in
+        grad_ref[rows] = grad_ref[rows] + inner
+
+    for copy in to_west + to_east:
+        copy.wait_send()
 
     @pl.when(top)
     def _():
@@ -528,6 +538,18 @@
         copy.wait_send()
     for copy in z_copies:
         copy.wait_send()
+
+
+def write_out(eta_ref, grad_ref, eta_hbm, grad_hbm, sem):
+    copies = []
+    for index, (src, dst) in enumerate(((eta_ref, eta_hbm), (grad_ref, grad_hbm))):
+        for part in range(4):
+            rows = pl.ds(part * 128, 128)
+            copies.append(pltpu.make_async_copy(src.at[rows], dst.at[rows], sem.at[index, part]))
+    for copy in copies:
+        copy.start()
+    for copy in copies:
+        copy.wait()
 
 
 def local(
@@ -540,7 +562,7 @@
     vmem = pl.BlockSpec(memory_space=pltpu.VMEM)
     dma = pltpu.SemaphoreType.DMA
     block = jax.ShapeDtypeStruct((512, 128), F32)
-    return pl.pallas_call(
+    eta, gradient = pl.pallas_call(
         functools.partial(kernel, nlon, nlat),
         out_shape=(block, block),
         in_specs=[hbm] * 8,
@@ -553,8 +575,8 @@
             pltpu.VMEM((2, 544, 128), F32),
             pltpu.VMEM((2, 544, 128), F32),
             pltpu.VMEM((512, 128), F32),
-            pltpu.VMEM((8, 2, 8, 512), F32),
-            pltpu.VMEM((8, 2, 8, 512), F32),
+            pltpu.VMEM((4, 8, 2, 8, 128), F32),
+            pltpu.VMEM((4, 8, 2, 8, 128), F32),
             pltpu.VMEM((4, 8, 128), F32),
             pltpu.VMEM((4, 128), F32),
             pltpu.VMEM((512, 256), F32),
@@ -563,9 +585,10 @@
             pltpu.VMEM((512, 256), F32),
             pltpu.VMEM((XG, 8, 128), F32),
             pltpu.VMEM((nz, 8, 128), F32),
+            pltpu.VMEM((nz, 8, 128), F32),
             dma((8,)),
-            dma((8,)),
-            dma((8,)),
+            dma((16,)),
+            dma((16,)),
             dma((XG - 1,)),
             dma((XG - 1,)),
             dma((nz - 1,)),
@@ -584,6 +607,14 @@
         obs_weight,
         smooth_scale.reshape(4, 128),
     )
+    return pl.pallas_call(
+        write_out,
+        out_shape=(block, block),
+        in_specs=[vmem] * 2,
+        out_specs=(hbm, hbm),
+        scratch_shapes=[dma((2, 4))],
+        compiler_params=pltpu.CompilerParams(vmem_limit_bytes=1024 * 1024),
+    )(eta, gradient)
 
 
 def solution(mesh):

time: 39.4 us -> 38.4 us (0.975)
  local copies, waits for them, and re-layouts: 2.08 us -> 0.67 us
  Pallas kernels: 36.5 us -> 36.9 us
    unnamed x4 -> x2, local copies, waits for them, and re-layouts: 2.08 us -> 0.67 us
    pallas_call x0 -> x1, Pallas kernels: none -> 0.85 us  [local(): pl.pallas_call(write_out, out_shape=(block, block), in_specs=[vmem] * 2,...]
    pallas_call x1, Pallas kernels: 36.5 us -> 36.1 us  [local(): pl.pallas_call(functools.partial(kernel, nlon, nlat), out_shape=(block, b...]
where the time goes in v3:
time: 38.4 us; the launch traced here: 38.3 us
  Pallas kernels  36.9 us (96%)
  local copies, waits for them, and re-layouts  0.67 us (2%)
  between operations  0.65 us (2%)
    pallas_call x1, Pallas kernels, local(): pl.pallas_call(functools.partial(kernel, nlon, nlat), out_shape=(block, b...  36.1 us
    pallas_call x1, Pallas kernels, local(): pl.pallas_call(write_out, out_shape=(block, block), in_specs=[vmem] * 2,...  0.85 us

profile of v3, /device:TPU:26, one launch (start us, length us, event | category | flops | bytes accessed | tf_op | source)
XLA Modules:
  0.0 38.3 jit_solution(16472091607144123037)
XLA Ops:
  0.6 0.0 copy-start
  0.6 0.7 %copy-done = f32[512]{0:T(512)S(1)} copy-done((f32[512]{0:T(512)S(1)}, f32[512]{0:T(512)}, u32[]{:S(2)}) %copy-start) | copy-done | bytes 2072
  1.3 36.1 %shard_map.95 = (f32[512,128]{1,0:T(8,128)S(1)}, f32[512,128]{1,0:T(8,128)S(1)}) custom-call(s32[512,128]{1,0:T(8,128)} %wet_hbm.1, s32[512,128]{1,0:T(8,128)} %east_hbm.1, s32[512,128]{1,0:T(8,128)} %north_hbm.1, f32[512,128]{1,0:T(8,128)} %cour_hbm.1, f32[512,128]{1,0:T(8,128)} %incr_hbm.1, f32[512,128]{1,0:T(8,128)} %innov_hbm.1, f32[512,128]{1,0:T(8,128)} %ow_hbm.1, ...), custom_call_target="tpu_custom_call" | custom-call | tf_op jit(solution)/shard_map/pallas_call | solution.py:565
  37.4 0.9 %shard_map.96 = (f32[512,128]{1,0:T(8,128)}, f32[512,128]{1,0:T(8,128)}) custom-call(f32[512,128]{1,0:T(8,128)S(1)} %get-tuple-element.4.eta_ref, f32[512,128]{1,0:T(8,128)S(1)} %get-tuple-element.5.grad_ref), custom_call_target="tpu_custom_call" | custom-call | tf_op jit(solution)/shard_map/pallas_call | solution.py:610
Async XLA Ops:
  0.6 0.7 %copy-start = (f32[512]{0:T(512)S(1)}, f32[512]{0:T(512)}, u32[]{:S(2)}) copy-start(f32[512]{0:T(512)} %param.15) | copy-start | bytes 6148

commit v4 on v3

--- a/solution.py
+++ b/solution.py
@@ -76,6 +76,7 @@
     xbuf,
     zbuf,
     z_weight,
+    known,
     in_sem,
     hs,
     hr,
@@ -155,7 +156,7 @@
     for load in loads:
         load.start()
     far_first = sorted(range(1, nz), key=lambda step: -min(step, nz - step))
-    for step in far_first:
+    for step in (1, nz - 1):
         greet(z_peer(step), lat)
     for step in range(1, XG):
         greet(x_peer(step), lat)
@@ -205,12 +206,30 @@
                 joined = jnp.where(slot == index + 1, moved, joined)
             packed[rows] = joined
 
-    links = 2 + (XG - 1) + (nz - 1)
+    links = 2 + (XG - 1) + 2
     north_links = jnp.where(
         top, 3 - ne_self.astype(jnp.int32) - nw_self.astype(jnp.int32), 3
     )
     south_links = jnp.where(low, 0, 3)
     pl.semaphore_wait(barrier, links + north_links + south_links)
+
+    rounds = nz.bit_length() - 2
+
+    def pass_on(index):
+        for step in (2**index, nz - 2**index):
+            pl.semaphore_signal(
+                known.at[index],
+                inc=1,
+                device_id={"lon": z_peer(step), "lat": lat},
+                device_id_type=pl.DeviceIdType.MESH,
+            )
+
+    def hear(index):
+        pl.semaphore_wait(known.at[index], 2)
+        if index + 1 < rounds:
+            pass_on(index + 1)
+
+    pass_on(0)
 
     top_rows = main.at[pl.ds(0, FIELDS), pl.ds(PAD + 504, 8)]
     low_rows = main.at[pl.ds(0, FIELDS), pl.ds(PAD, 8)]
@@ -300,6 +319,8 @@
     for row in range(8, 536, RH):
         delta[0, pl.ds(row, RH)] = jnp.zeros((RH, 128), F32)
         delta[1, pl.ds(row, RH)] = jnp.zeros((RH, 128), F32)
+
+    hear(0)
 
     first_half = lax.rem(lane8, 16) < 8
     def set_west(rows, outer):
@@ -420,6 +441,9 @@
             delta[side, here] = start
     eta_ref[...] = main[0, pl.ds(PAD, 512)]
 
+    if rounds > 1:
+        hear(1)
+
     def adjoint_pair(step, carry):
         substep(side_b, side_a)
         substep(side_a, side_b)
@@ -474,6 +498,8 @@
         remote(zbuf.at[0], zbuf.at[step], zs.at[step - 1], zr.at[step - 1], z_peer(step), lat)
         for step in far_first
     ]
+    for index in range(2, rounds):
+        hear(index)
     for copy in z_copies:
         copy.start()
 
@@ -558,6 +584,16 @@
     nlon = lax.axis_size("lon")
     nlat = lax.axis_size("lat")
     nz = nlon // XG
+    inputs = (
+        wet_mask,
+        east_level,
+        north_level,
+        courant,
+        increment,
+        innovation,
+        obs_weight,
+        smooth_scale.reshape(4, 128),
+    )
     hbm = pl.BlockSpec(memory_space=pltpu.MemorySpace.HBM)
     vmem = pl.BlockSpec(memory_space=pltpu.VMEM)
     dma = pltpu.SemaphoreType.DMA
@@ -586,6 +622,7 @@
             pltpu.VMEM((XG, 8, 128), F32),
             pltpu.VMEM((nz, 8, 128), F32),
             pltpu.VMEM((nz, 8, 128), F32),
+            pltpu.SemaphoreType.REGULAR((nz.bit_length() - 2,)),
             dma((8,)),
             dma((16,)),
             dma((16,)),
@@ -595,18 +632,9 @@
             dma((nz - 1,)),
         ],
         compiler_params=pltpu.CompilerParams(
-            collective_id=0, has_side_effects=True, vmem_limit_bytes=54656 * 1024
+            collective_id=0, has_side_effects=True, vmem_limit_bytes=32 * 1024 * 1024
         ),
-    )(
-        wet_mask,
-        east_level,
-        north_level,
-        courant,
-        increment,
-        innovation,
-        obs_weight,
-        smooth_scale.reshape(4, 128),
-    )
+    )(*[pltpu.with_memory_space_constraint(value, pltpu.MemorySpace.HBM) for value in inputs])
     return pl.pallas_call(
         write_out,
         out_shape=(block, block),

time: 38.4 us -> 36.6 us (0.953)
  the two profiles are of different devices: /device:TPU:26 before, /device:TPU:25 now
where the time goes in v4:
time: 36.6 us; the launch traced here: 36.4 us
  Pallas kernels  35.8 us (98%)
  between operations  0.64 us (2%)
    pallas_call x1, Pallas kernels, local(): pl.pallas_call(functools.partial(kernel, nlon, nlat), out_shape=(block, b...  35 us
    pallas_call x1, Pallas kernels, local(): pl.pallas_call(write_out, out_shape=(block, block), in_specs=[vmem] * 2,...  0.85 us

profile of v4, /device:TPU:25, one launch (start us, length us, event | category | flops | bytes accessed | tf_op | source)
XLA Modules:
  0.0 36.4 jit_solution(8914569107379201143)
XLA Ops:
  0.6 35.0 %shard_map.95 = (f32[512,128]{1,0:T(8,128)S(1)}, f32[512,128]{1,0:T(8,128)S(1)}) custom-call(s32[512,128]{1,0:T(8,128)} %wet_hbm.1, s32[512,128]{1,0:T(8,128)} %east_hbm.1, s32[512,128]{1,0:T(8,128)} %north_hbm.1, f32[512,128]{1,0:T(8,128)} %cour_hbm.1, f32[512,128]{1,0:T(8,128)} %incr_hbm.1, f32[512,128]{1,0:T(8,128)} %innov_hbm.1, f32[512,128]{1,0:T(8,128)} %ow_hbm.1, ...), custom_call_target="tpu_custom_call" | custom-call | tf_op jit(solution)/shard_map/pallas_call | solution.py:601
  35.6 0.9 %shard_map.96 = (f32[512,128]{1,0:T(8,128)}, f32[512,128]{1,0:T(8,128)}) custom-call(f32[512,128]{1,0:T(8,128)S(1)} %get-tuple-element.4.eta_ref, f32[512,128]{1,0:T(8,128)S(1)} %get-tuple-element.5.grad_ref), custom_call_target="tpu_custom_call" | custom-call | tf_op jit(solution)/shard_map/pallas_call | solution.py:638

commit v5 on v4

--- a/solution.py
+++ b/solution.py
@@ -412,7 +412,7 @@
             states = [src[side][here] for side in range(2)]
             east = [roll(state, -1, 1) for state in states]
             west = [roll(state, 1, 1) for state in states]
-            for side, field in enumerate((main, halo)):
+            for side, field in enumerate((main, halo)[: 2 if dst else 1]):
                 state = states[side]
                 to_east = jnp.where(last_lane, east[1 - side], east[side]) - state
                 to_west = jnp.where(zero_lane, west[1 - side], west[side]) - state
@@ -421,7 +421,8 @@
                 spread = spread + field[3, down] * (src[side][down] - state)
                 change = delta[side, here] + field[1, here] * spread
                 delta[side, here] = change
-                dst[side][here] = state + change
+                if dst:
+                    dst[side][here] = state + change
 
     side_a = (main.at[0], halo.at[0])
     side_b = (work.at[0], work.at[1])
@@ -436,10 +437,14 @@
     for row in range(8, 536, RH):
         here = pl.ds(row, RH)
         for side, field in enumerate((main, halo)):
-            start = field[1, here] * field[4, here] * (field[0, here] - field[5, here])
+            height = field[0, here]
+            start = field[1, here] * field[4, here] * (height - field[5, here])
+            if side == 0:
+                low_end, high_end = max(row, PAD), min(row + RH, PAD + 512)
+                own = height[low_end - row : high_end - row]
+                eta_ref[pl.ds(low_end - PAD, high_end - low_end)] = own
             work[side, here] = start
             delta[side, here] = start
-    eta_ref[...] = main[0, pl.ds(PAD, 512)]
 
     if rounds > 1:
         hear(1)
@@ -449,7 +454,9 @@
         substep(side_a, side_b)
         return carry
 
-    lax.fori_loop(0, SUBSTEPS // 2, adjoint_pair, 0)
+    lax.fori_loop(0, SUBSTEPS // 2 - 1, adjoint_pair, 0)
+    substep(side_b, side_a)
+    substep(side_a, None)
 
     ends = jnp.zeros((8, 128), F32)
     pick_row = iota((8, 256), 0)
@@ -569,8 +576,8 @@
 def write_out(eta_ref, grad_ref, eta_hbm, grad_hbm, sem):
     copies = []
     for index, (src, dst) in enumerate(((eta_ref, eta_hbm), (grad_ref, grad_hbm))):
-        for part in range(4):
-            rows = pl.ds(part * 128, 128)
+        for part in range(2):
+            rows = pl.ds(part * 256, 256)
             copies.append(pltpu.make_async_copy(src.at[rows], dst.at[rows], sem.at[index, part]))
     for copy in copies:
         copy.start()
@@ -640,7 +647,7 @@
         out_shape=(block, block),
         in_specs=[vmem] * 2,
         out_specs=(hbm, hbm),
-        scratch_shapes=[dma((2, 4))],
+        scratch_shapes=[dma((2, 2))],
         compiler_params=pltpu.CompilerParams(vmem_limit_bytes=1024 * 1024),
     )(eta, gradient)
 

time: 36.6 us -> 36.2 us (0.989)
  Pallas kernels: 35.8 us -> 35.4 us
where the time goes in v5:
time: 36.2 us; the launch traced here: 36.1 us
  Pallas kernels  35.4 us (98%)
  between operations  0.64 us (2%)
    pallas_call x1, Pallas kernels, local(): pl.pallas_call(functools.partial(kernel, nlon, nlat), out_shape=(block, b...  34.6 us
    pallas_call x1, Pallas kernels, local(): pl.pallas_call(write_out, out_shape=(block, block), in_specs=[vmem] * 2,...  0.82 us

profile of v5, /device:TPU:25, one launch (start us, length us, event | category | flops | bytes accessed | tf_op | source)
XLA Modules:
  0.0 36.1 jit_solution(17092034362017244360)
XLA Ops:
  0.6 34.6 %shard_map.95 = (f32[512,128]{1,0:T(8,128)S(1)}, f32[512,128]{1,0:T(8,128)S(1)}) custom-call(s32[512,128]{1,0:T(8,128)} %wet_hbm.1, s32[512,128]{1,0:T(8,128)} %east_hbm.1, s32[512,128]{1,0:T(8,128)} %north_hbm.1, f32[512,128]{1,0:T(8,128)} %cour_hbm.1, f32[512,128]{1,0:T(8,128)} %incr_hbm.1, f32[512,128]{1,0:T(8,128)} %innov_hbm.1, f32[512,128]{1,0:T(8,128)} %ow_hbm.1, ...), custom_call_target="tpu_custom_call" | custom-call | tf_op jit(solution)/shard_map/pallas_call | solution.py:608
  35.2 0.8 %shard_map.96 = (f32[512,128]{1,0:T(8,128)}, f32[512,128]{1,0:T(8,128)}) custom-call(f32[512,128]{1,0:T(8,128)S(1)} %get-tuple-element.4.eta_ref, f32[512,128]{1,0:T(8,128)S(1)} %get-tuple-element.5.grad_ref), custom_call_target="tpu_custom_call" | custom-call | tf_op jit(solution)/shard_map/pallas_call | solution.py:645
